TPU v7x, 32 devices: a whole 2x2x4 slice. The times are simulated.
32 devices in a mesh: shard: 2 (over y), rep: 16 (over z, x, core).
Axes of the slice: x: 2, y: 2, z: 4, core: 2. Of those that a mesh axis runs over, the one named last changes fastest.
Arguments:
- layer_in: bfloat16 [32768, 768], P(('shard', 'rep')), may hold values from -6 to 6
- segment_ids: int32 [32, 1024], P(('shard', 'rep')), may hold values from 0 to 2, never falling along the last dimension, each value on 1 to 512 neighbouring positions
- cotangent: bfloat16 [32768, 768], P(('shard', 'rep')), may hold values from -6 to 6
- norm_gain: bfloat16 [768], P('shard'), may hold values from 0.5 to 1.5
- in_weight: bfloat16 [768, 3352], P('shard'), may hold values from -0.21875 to 0.21875
- conv_weight: bfloat16 [4, 1792], P(None, 'shard'), may hold values from -3 to 3
- conv_bias: bfloat16 [1792], P('shard'), may hold values from -0.5 to 0.5
- dt_bias: bfloat16 [24], P('shard'), may hold values from -7 to -3
- a_log: bfloat16 [24], P('shard'), may hold values from 0 to 2.765625
- skip_gain: bfloat16 [24], P('shard'), may hold values from 0.5 to 1.5
- gate_gain: bfloat16 [1536], P('shard'), may hold values from 0.5 to 1.5
- out_weight: bfloat16 [1536, 768], P('shard'), may hold values from -0.15625 to 0.15625
Outputs:
- layer_out: bfloat16 [32768, 768], P(('shard', 'rep'))
- input_grad: bfloat16 [32768, 768], P(('shard', 'rep'))
- norm_gain_grad: float32 [768], P('shard')
- in_weight_grad: float32 [768, 3352], P('shard')
- conv_weight_grad: float32 [4, 1792], P(None, 'shard')
- conv_bias_grad: float32 [1792], P('shard')
- dt_bias_grad: float32 [24], P('shard')
- a_log_grad: float32 [24], P('shard')
- skip_grad: float32 [24], P('shard')
- gate_gain_grad: float32 [1536], P('shard')
- out_weight_grad: float32 [1536, 768], P('shard')
Inputs may be any that keep to these rules, and one draw needn't show every extreme that they name: `segment_ids`: within each row the numbers never fall; a document spans 1 to 512 tokens and some document in each row spans exactly that.
All inputs are finite; a program needn't handle non-finite values.
Results may differ from a plain program's by a relative error of at most 0.012.
Values may be sent and summed in bfloat16 or wider, within the bound.
A program may use at most 192 MiB of HBM per device.

v0:
```python
import jax
import jax.numpy as jnp
from jax import lax
from jax.sharding import PartitionSpec as P

HEADS = 24
HEADDIM = 64
STATE = 128
CONV = 4
STRETCH = 256
INNER = 1536
XBC = 1792


eps = 1e-05
highest = lax.Precision.HIGHEST


def block_step(carry_in, inputs):
    hidden, last_segment = carry_in
    values_flat, b_rows, c_rows, step_t, decay_t, segment = inputs
    length = segment.shape[0]
    values = values_flat.reshape(length, HEADS, HEADDIM)
    running_t = jnp.cumsum(decay_t, axis=1)
    position = jnp.arange(length)
    allowed = (position[:, None] >= position[None, :]) & (segment[:, None] == segment[None, :])
    spread_log = jnp.where(allowed[None], running_t[:, :, None] - running_t[:, None, :], -1e30)
    kernel = jnp.exp(spread_log)
    pair_scores = jnp.dot(c_rows, b_rows.T, precision=highest)
    weighted = values * step_t.T[:, :, None]
    local_part = jnp.einsum("hts,shp->thp", kernel * pair_scores[None], weighted, precision=highest)
    keep_in = (segment == last_segment).astype(jnp.float32)
    entering = jnp.exp(running_t) * keep_in[None, :]
    carried_part = (
        jnp.einsum("tn,hpn->thp", c_rows, hidden, precision=highest) * entering.T[:, :, None]
    )
    keep_end = (segment == segment[-1]).astype(jnp.float32)
    leaving = jnp.exp(running_t[:, -1:] - running_t) * keep_end[None, :]
    carried = jnp.exp(running_t[:, -1]) * (segment[-1] == last_segment).astype(jnp.float32)
    new_state = hidden * carried[:, None, None] + jnp.einsum(
        "shp,sn->hpn", weighted * leaving.T[:, :, None], b_rows, precision=highest
    )
    return ((new_state, segment[-1]), (local_part + carried_part).reshape(length, HEADS * HEADDIM))


def state_scan(values, b_rows, c_rows, step_sizes, decay_log, segment):
    length = segment.shape[0]
    blocks = length // STRETCH
    inputs = (
        values.reshape(blocks, STRETCH, HEADS * HEADDIM),
        b_rows.reshape(blocks, STRETCH, STATE),
        c_rows.reshape(blocks, STRETCH, STATE),
        jnp.transpose(step_sizes.reshape(blocks, STRETCH, HEADS), (0, 2, 1)),
        jnp.transpose(decay_log.reshape(blocks, STRETCH, HEADS), (0, 2, 1)),
        segment.reshape(blocks, STRETCH),
    )
    start = (jnp.zeros((HEADS, HEADDIM, STATE), jnp.float32), jnp.array(-1, jnp.int32))
    ending, outputs = lax.scan(jax.checkpoint(block_step), start, inputs)
    return outputs.reshape(length, HEADS, HEADDIM)


def middle(projected, conv_w, conv_b, step_bias, alog, skip, gate_vec, segment):
    length = segment.shape[0]
    gate_part = projected[:, :INNER]
    conv_input = projected[:, INNER : INNER + XBC]
    raw_step = projected[:, INNER + XBC :]
    convolved = jnp.zeros((length, XBC), jnp.float32) + conv_b[None, :]
    for offset in range(CONV):
        shifted = jnp.pad(conv_input, ((offset, 0), (0, 0)))[:length]
        shifted_seg = jnp.pad(segment, (offset, 0), constant_values=-1)[:length]
        same_doc = (shifted_seg == segment).astype(jnp.float32)
        convolved = convolved + conv_w[CONV - 1 - offset][None, :] * shifted * same_doc[:, None]
    active = jax.nn.silu(convolved)
    values = active[:, :INNER].reshape(length, HEADS, HEADDIM)
    b_rows = active[:, INNER : INNER + STATE]
    c_rows = active[:, INNER + STATE :]
    step_sizes = jax.nn.softplus(raw_step + step_bias[None, :])
    decay_log = -jnp.exp(alog)[None, :] * step_sizes
    outputs = (
        state_scan(values, b_rows, c_rows, step_sizes, decay_log, segment)
        + skip[None, :, None] * values
    )
    gated = outputs.reshape(length, INNER) * jax.nn.silu(gate_part)
    inv_rms = lax.rsqrt(jnp.mean(gated * gated, axis=-1, keepdims=True) + eps)
    return gated * inv_rms * gate_vec[None, :]


def normalize(features, gain_vec):
    inv_rms = lax.rsqrt(jnp.mean(features * features, axis=-1, keepdims=True) + eps)
    return features * inv_rms * gain_vec[None, :]


def body(
    layer_in,
    segment_ids,
    cotangent,
    norm_gain,
    in_weight,
    conv_weight,
    conv_bias,
    dt_bias,
    a_log,
    skip_gain,
    gate_gain,
    out_weight,
):
    shards = (
        norm_gain,
        in_weight,
        conv_weight,
        conv_bias,
        dt_bias,
        a_log,
        skip_gain,
        gate_gain,
        out_weight,
    )
    gathered = (
        lax.all_gather(shards[0], "shard", axis=0, tiled=True),
        lax.all_gather(shards[1], "shard", axis=0, tiled=True),
        lax.all_gather(shards[2], "shard", axis=1, tiled=True),
        lax.all_gather(shards[3], "shard", axis=0, tiled=True),
        lax.all_gather(shards[4], "shard", axis=0, tiled=True),
        lax.all_gather(shards[5], "shard", axis=0, tiled=True),
        lax.all_gather(shards[6], "shard", axis=0, tiled=True),
        lax.all_gather(shards[7], "shard", axis=0, tiled=True),
        lax.all_gather(shards[8], "shard", axis=0, tiled=True),
    )
    (
        full_gain,
        full_in,
        full_conv,
        full_bias,
        full_step,
        full_alog,
        full_skip,
        full_gate,
        full_out,
    ) = gathered
    segment = segment_ids.reshape(-1)
    inputs_f = layer_in.astype(jnp.float32)
    normed, norm_pull = jax.vjp(normalize, inputs_f, full_gain.astype(jnp.float32))
    normed_low = normed.astype(jnp.bfloat16)
    projected = jnp.dot(normed_low, full_in, preferred_element_type=jnp.float32)
    small_params = tuple(
        (
            p.astype(jnp.float32)
            for p in (full_conv, full_bias, full_step, full_alog, full_skip, full_gate)
        )
    )

    def middle_local(rows_in, conv_w, conv_b, step_bias, alog, skip, gate_vec):
        return middle(rows_in, conv_w, conv_b, step_bias, alog, skip, gate_vec, segment)

    mixed, mid_pull = jax.vjp(middle_local, projected, *small_params)
    mixed_low = mixed.astype(jnp.bfloat16)
    layer_out = (
        inputs_f + jnp.dot(mixed_low, full_out, preferred_element_type=jnp.float32)
    ).astype(jnp.bfloat16)
    out_grad = jnp.einsum("ti,td->id", mixed_low, cotangent, preferred_element_type=jnp.float32)
    mixed_grad = jnp.einsum("td,id->ti", cotangent, full_out, preferred_element_type=jnp.float32)
    mid_grads = mid_pull(mixed_grad)
    proj_grad = mid_grads[0].astype(jnp.bfloat16)
    in_grad = jnp.einsum("td,tp->dp", normed_low, proj_grad, preferred_element_type=jnp.float32)
    normed_grad = jnp.einsum("tp,dp->td", proj_grad, full_in, preferred_element_type=jnp.float32)
    input_part, gain_grad = norm_pull(normed_grad)
    input_grad = (cotangent.astype(jnp.float32) + input_part).astype(jnp.bfloat16)
    factor = 1.0 / (lax.axis_size("shard") * lax.axis_size("rep"))
    gradients = (
        gain_grad,
        in_grad,
        mid_grads[1],
        mid_grads[2],
        mid_grads[3],
        mid_grads[4],
        mid_grads[5],
        mid_grads[6],
        out_grad,
    )
    grouped = (
        lax.psum_scatter(gradients[0], "shard", scatter_dimension=0, tiled=True),
        lax.psum_scatter(gradients[1], "shard", scatter_dimension=0, tiled=True),
        lax.psum_scatter(gradients[2], "shard", scatter_dimension=1, tiled=True),
        lax.psum_scatter(gradients[3], "shard", scatter_dimension=0, tiled=True),
        lax.psum_scatter(gradients[4], "shard", scatter_dimension=0, tiled=True),
        lax.psum_scatter(gradients[5], "shard", scatter_dimension=0, tiled=True),
        lax.psum_scatter(gradients[6], "shard", scatter_dimension=0, tiled=True),
        lax.psum_scatter(gradients[7], "shard", scatter_dimension=0, tiled=True),
        lax.psum_scatter(gradients[8], "shard", scatter_dimension=0, tiled=True),
    )
    summed = lax.psum(
        (
            grouped[0],
            grouped[1],
            grouped[2],
            grouped[3],
            grouped[4],
            grouped[5],
            grouped[6],
            grouped[7],
            grouped[8],
        ),
        "rep",
    )
    averaged = tuple((item * factor for item in summed))
    return (
        layer_out,
        input_grad,
        averaged[0],
        averaged[1],
        averaged[2],
        averaged[3],
        averaged[4],
        averaged[5],
        averaged[6],
        averaged[7],
        averaged[8],
    )


def solution(mesh):
    in_specs = (
        P(("shard", "rep"), None),
        P(("shard", "rep"), None),
        P(("shard", "rep"), None),
        P("shard"),
        P("shard", None),
        P(None, "shard"),
        P("shard"),
        P("shard"),
        P("shard"),
        P("shard"),
        P("shard"),
        P("shard", None),
    )
    out_specs = (
        P(("shard", "rep"), None),
        P(("shard", "rep"), None),
        P("shard"),
        P("shard", None),
        P(None, "shard"),
        P("shard"),
        P("shard"),
        P("shard"),
        P("shard"),
        P("shard"),
        P("shard", None),
    )
    return jax.shard_map(body, mesh=mesh, in_specs=in_specs, out_specs=out_specs, check_vma=False)
```

profile of v0, /device:TPU:0, one launch (start us, length us, event | category | flops | bytes accessed | tf_op | source)
XLA Modules:
  0.0 1228.4 jit_solution(13617543200799316161)
XLA Ops:
  11.8 5.2 all-gather
  21.7 5.0 all-reduce.33
  27.3 4.8 all_gather.32
  33.8 4.4 all-gather.1
  40.9 4.4 all-gather.2
  45.3 34.8 %all-gather.6.cloned.1.call-done = bf16[768,3352]{0,1:T(8,128)(2,1)} async-done(((bf16[384,3352]{0,1:T(8,128)(2,1)}), bf16[768,3352]{0,1:T(8,128)(2,1)}) %all-gather.6.cloned.1.call-update) | async-done | bytes 5148688 | tf_op jit(solution)/shard_map/all_gather | solution.py:120
  80.2 11.8 fusion.103
  96.0 9.5 fusion.86
  112.4 6.1 copy.224
  124.0 260.5 %while.45 = (s32[]{:T(128)}, f32[24,64,128]{2,1,0:T(8,128)S(1)}, s32[]{:T(128)}, f32[4,256,1536]{1,0,2:T(4,128)}, f32[4,24,64,128]{3,2,1,0:T(8,128)}, /*index=5*...) while((s32[]{:T(128)}, f32[24,64,128]{2,1,0:T(8,128)S(1)}, ...), condition=%wide.region_4.5_spmd.clone, body=%wide.region_1.4_spmd.clone.sunk | while | flops 2525258752 | bytes 24490912 | solution.py:58
  131.3 8.1 fusion.198
  142.3 7.7 copy.243
  150.0 34.3 %dynamic_update_slice.87 = f32[4,256,1536]{1,0,2:T(4,128)} dynamic-update-slice(f32[4,256,1536]{1,0,2:T(4,128)} %get-tuple-element.1095, f32[1,256,1536]{1,0,2:T(1,128)} %copy.243, s32[]{:T(128)} %get-tuple-element.1092, s32[]{:T(128)} %constant.145.clone.1..sunk, s32[]{:T(128)} %constant.145.clone.1..sunk) | dynamic-update-slice | bytes 3145732 | tf_op jit(solution)/shard_map/jvp()/while/body/jit(dynamic_update_index_in_dim)/dynamic_update_slice | solution.py:58
  196.4 8.1 fusion.198
  207.4 7.7 copy.243
  215.1 34.3 %dynamic_update_slice.87 = f32[4,256,1536]{1,0,2:T(4,128)} dynamic-update-slice(f32[4,256,1536]{1,0,2:T(4,128)} %get-tuple-element.1095, f32[1,256,1536]{1,0,2:T(1,128)} %copy.243, s32[]{:T(128)} %get-tuple-element.1092, s32[]{:T(128)} %constant.145.clone.1..sunk, s32[]{:T(128)} %constant.145.clone.1..sunk) | dynamic-update-slice | bytes 3145732 | tf_op jit(solution)/shard_map/jvp()/while/body/jit(dynamic_update_index_in_dim)/dynamic_update_slice | solution.py:58
  261.4 8.1 fusion.198
  272.5 7.7 copy.243
  280.2 34.3 %dynamic_update_slice.87 = f32[4,256,1536]{1,0,2:T(4,128)} dynamic-update-slice(f32[4,256,1536]{1,0,2:T(4,128)} %get-tuple-element.1095, f32[1,256,1536]{1,0,2:T(1,128)} %copy.243, s32[]{:T(128)} %get-tuple-element.1092, s32[]{:T(128)} %constant.145.clone.1..sunk, s32[]{:T(128)} %constant.145.clone.1..sunk) | dynamic-update-slice | bytes 3145732 | tf_op jit(solution)/shard_map/jvp()/while/body/jit(dynamic_update_index_in_dim)/dynamic_update_slice | solution.py:58
  326.5 8.1 fusion.198
  337.5 7.7 copy.243
  345.2 34.3 %dynamic_update_slice.87 = f32[4,256,1536]{1,0,2:T(4,128)} dynamic-update-slice(f32[4,256,1536]{1,0,2:T(4,128)} %get-tuple-element.1095, f32[1,256,1536]{1,0,2:T(1,128)} %copy.243, s32[]{:T(128)} %get-tuple-element.1092, s32[]{:T(128)} %constant.145.clone.1..sunk, s32[]{:T(128)} %constant.145.clone.1..sunk) | dynamic-update-slice | bytes 3145732 | tf_op jit(solution)/shard_map/jvp()/while/body/jit(dynamic_update_index_in_dim)/dynamic_update_slice | solution.py:58
  384.5 4.3 copy.201
  388.9 8.3 multiply_reduce_fusion.12
  399.7 4.9 fusion.118
  404.7 7.6 multiply_reduce_fusion.9
  412.3 14.6 %multiply_reduce_fusion.10 = (f32[1536]{0:T(1024)}, f32[1024,1536]{0,1:T(8,128)}, f32[1024,1536]{0,1:T(8,128)}) fusion(f32[1024,1792]{0,1:T(8,128)} %copy-done, f32[1024,3352]{0,1:T(8,128)} %fusion.103, f32[1024,1536]{0,1:T(8,128)S(1)} %copy-done.5, f32[1024]{0:T(1024)S(1)} %multiply_multiply_fusion.4, f32[1024]{0:T(1024)S(1)} %fusion.115, ...), kind=kLoop, calls=%fused_computation.162 | loop fusion | flops 33028608 | bytes 44066816 | tf_op jit(solution)/shard_map/transpose(jvp())/reduce_sum | solution.py:81
  426.9 8.1 reshape.529
  441.2 398.7 %while.46 = (s32[]{:T(128)}, f32[24,64,128]{2,1,0:T(8,128)}, f32[4,256,1536]{1,0,2:T(4,128)}, f32[4,256,128]{2,1,0:T(8,128)}, f32[4,256,128]{2,1,0:T(8,128)}, /*...) while((s32[]{:T(128)}, f32[24,64,128]{2,1,0:T(8,128)}, ...), condition=%wide.region_20.21_spmd.clone, body=%wide.region_7.20_spmd.clone.sunk | while | flops 5765438464 | bytes 55433972 | solution.py:58
  441.4 4.4 constant_dynamic-slice_fusion.11
  459.5 8.1 multiply_reduce_fusion.19
  470.5 10.5 fusion.220
  489.2 4.1 fusion.225
  495.5 7.6 copy.252
  503.1 34.3 %dynamic_update_slice.93 = f32[4,256,1536]{1,0,2:T(4,128)} dynamic-update-slice(f32[4,256,1536]{1,0,2:T(4,128)} %get-tuple-element.1146, f32[1,256,1536]{1,0,2:T(1,128)} %copy.252, s32[]{:T(128)S(6)} %sub.238, s32[]{:T(128)} %constant.145.clone.1..sunk.1, s32[]{:T(128)} %constant.145.clone.1..sunk.1) | dynamic-update-slice | bytes 3145732 | tf_op jit(solution)/shard_map/transpose(jvp())/while/body/jit(dynamic_update_index_in_dim)/dynamic_update_slice | solution.py:58
  540.3 4.2 constant_dynamic-slice_fusion.11
  559.2 8.1 multiply_reduce_fusion.19
  570.3 10.5 fusion.220
  595.2 7.6 copy.252
  602.9 34.3 %dynamic_update_slice.93 = f32[4,256,1536]{1,0,2:T(4,128)} dynamic-update-slice(f32[4,256,1536]{1,0,2:T(4,128)} %get-tuple-element.1146, f32[1,256,1536]{1,0,2:T(1,128)} %copy.252, s32[]{:T(128)S(6)} %sub.238, s32[]{:T(128)} %constant.145.clone.1..sunk.1, s32[]{:T(128)} %constant.145.clone.1..sunk.1) | dynamic-update-slice | bytes 3145732 | tf_op jit(solution)/shard_map/transpose(jvp())/while/body/jit(dynamic_update_index_in_dim)/dynamic_update_slice | solution.py:58
  640.1 4.2 constant_dynamic-slice_fusion.11
  659.0 8.1 multiply_reduce_fusion.19
  670.0 10.5 fusion.220
  695.0 7.6 copy.252
  702.6 34.3 %dynamic_update_slice.93 = f32[4,256,1536]{1,0,2:T(4,128)} dynamic-update-slice(f32[4,256,1536]{1,0,2:T(4,128)} %get-tuple-element.1146, f32[1,256,1536]{1,0,2:T(1,128)} %copy.252, s32[]{:T(128)S(6)} %sub.238, s32[]{:T(128)} %constant.145.clone.1..sunk.1, s32[]{:T(128)} %constant.145.clone.1..sunk.1) | dynamic-update-slice | bytes 3145732 | tf_op jit(solution)/shard_map/transpose(jvp())/while/body/jit(dynamic_update_index_in_dim)/dynamic_update_slice | solution.py:58
  739.8 4.2 constant_dynamic-slice_fusion.11
  758.7 8.1 multiply_reduce_fusion.19
  769.8 10.5 fusion.220
  794.7 7.6 copy.252
  802.4 34.3 %dynamic_update_slice.93 = f32[4,256,1536]{1,0,2:T(4,128)} dynamic-update-slice(f32[4,256,1536]{1,0,2:T(4,128)} %get-tuple-element.1146, f32[1,256,1536]{1,0,2:T(1,128)} %copy.252, s32[]{:T(128)S(6)} %sub.238, s32[]{:T(128)} %constant.145.clone.1..sunk.1, s32[]{:T(128)} %constant.145.clone.1..sunk.1) | dynamic-update-slice | bytes 3145732 | tf_op jit(solution)/shard_map/transpose(jvp())/while/body/jit(dynamic_update_index_in_dim)/dynamic_update_slice | solution.py:58
  841.8 7.2 copy.202
  854.7 8.0 multiply_add_fusion.1
  862.8 14.0 %multiply_reduce_fusion.8 = (f32[1792]{0:T(1024)S(1)}, f32[1792]{0:T(1024)S(1)}, f32[1792]{0:T(1024)S(1)}, f32[1792]{0:T(1024)S(1)}, f32[1792]{0:T(1024)S(1)}, /*index=5*/f32[1024,1792]{0,1:T(8,128)S(1)}) fusion(f32[1024,1792]{0,1:T(8,128)S(1)} %bitcast.362, f32[1024]{0:T(1024)S(1)} %copy-done.42, f32[1024]{0:T(1024)S(1)} %copy-done.40, ...), kind=kLoop, calls=%fused_computation.151 | loop fusion | flops 42196224 | bytes 36748288 | tf_op jit(solution)/shard_map/transpose(jvp())/reduce_sum | solution.py:72
  876.8 6.3 multiply_multiply_fusion
  883.1 11.3 fusion.83
  894.5 14.5 %fusion.101 = f32[768,3352]{0,1:T(8,128)} fusion(bf16[1024,768]{1,0:T(8,128)(2,1)S(1)} %copy-done.7, f32[768]{0:T(1024)S(1)} %copy-done.49, f32[1024]{0:T(1024)S(1)} %copy-done.51, f32[1024,1536]{0,1:T(8,128)} %get-tuple-element.822, f32[1024,1792]{0,1:T(8,128)} %fusion.83, f32[1024,24]{0,1:T(8,128)S(1)} %get-tuple-element.799), kind=kOutput, calls=%fused_computation.189 | convolution fusion | flops 5285683200 | bytes 25607168 | tf_op jit(solution)/shard_map/td,tp->dp/dot_general | solution.py:164
  913.1 116.8 %reduce-scatter.6.cloned.1.call-done = f32[384,3352]{0,1:T(8,128)} async-done(((f32[768,3352]{0,1:T(8,128)}), f32[384,3352]{0,1:T(8,128)}) %reduce-scatter.6.cloned.1.call-update) | async-done | bytes 5148688 | tf_op jit(solution)/shard_map/reduce_scatter | solution.py:182
  1030.0 12.3 %fusion.93 = (f32[768]{0:T(1024)S(1)}, f32[1024]{0:T(1024)S(1)}, f32[1024,768]{1,0:T(8,128)}) fusion(bf16[1024,768]{1,0:T(8,128)(2,1)S(1)} %copy-done.7, f32[1024]{0:T(1024)S(1)} %copy-done.51, f32[768]{0:T(1024)S(1)} %copy-done.49, bf16[768,3352]{0,1:T(8,128)(2,1)} %all-gather.6.cloned.1.call-done, f32[1024,1536]{0,1:T(8,128)} %get-tuple-element.822, ...), kind=kOutput, calls=%fused_computation.179 | convolution fusion | flops 5288040448 | bytes 23611392 | tf_op jit(solution)/shard_map/tp,dp->td/dot_general | solution.py:165
  1042.5 7.7 all-reduce.32
  1050.8 4.2 fusion.95
  1055.0 6.9 fusion.97
  1063.1 63.4 %all-reduce.30 = (f32[384]{0:T(512)S(1)}, f32[4,896]{1,0:T(4,128)S(1)}, f32[896]{0:T(1024)S(1)}, f32[12]{0:T(128)S(1)}, f32[12]{0:T(128)S(1)}, /*index=5*/f32[12]{0:T(128)S(1)}, f32[768]{0:T(1024)S(1)}) all-reduce(f32[384]{0:T(512)S(1)} %dynamic-slice.4, f32[4,896]{1,0:T(4,128)S(1)} %copy.153, ...), channel_id=1, replica_groups=mesh['shard'=2,'rep'=16] {'rep'}, use_global_device_ids=true, to_apply=%region_24.25 | all-reduce | flops 5668 | bytes 45344 | tf_op jit(solution)/shard_map/psum | solution.py:191
  1130.4 84.0 %all-reduce.36.cloned.1.call-done = (f32[384,3352]{0,1:T(8,128)}, f32[768,768]{1,0:T(8,128)}) async-done(((f32[384,3352]{0,1:T(8,128)}, f32[768,768]{1,0:T(8,128)}), (f32[384,3352]{0,1:T(8,128)}, f32[768,768]{1,0:T(8,128)})) %all-reduce.36.cloned.1.call-update) | async-done | bytes 7507984 | tf_op jit(solution)/shard_map/psum | solution.py:191
  1214.5 5.3 broadcast_multiply_fusion.1
  (584 shorter events, 238.2 us)
Async XLA Ops:
  7.2 73.0 %all-gather.6.cloned.1.call-start = ((), (), s32[]{:S(2)}) async-start(), calls=%async_computation.3 | async-start | bytes 7723008 | tf_op jit(solution)/shard_map/all_gather | solution.py:120
  7.9 396.8 %all-gather.8.cloned.1.call-start = ((), (), s32[]{:S(2)}) async-start(), calls=%async_computation.4 | async-start | bytes 3538944 | tf_op jit(solution)/shard_map/all_gather | solution.py:127
  8.7 904.4 %reduce-scatter.8.cloned.1.call-start = ((), (), s32[]{:S(2)}) async-start(), calls=%async_computation.6 | async-start | bytes 7077888 | tf_op jit(solution)/shard_map/reduce_scatter | solution.py:189
  11.1 80.8 %copy-start.50 = (f32[1024]{0:T(1024)}, f32[1024]{0:T(1024)S(1)}, u32[]{:S(2)}) copy-start(f32[1024]{0:T(1024)S(1)} %fusion.114) | copy-start | bytes 12292
  21.7 70.3 %copy-start.48 = (f32[768]{0:T(1024)}, f32[768]{0:T(1024)S(1)}, u32[]{:S(2)}) copy-start(f32[768]{0:T(1024)S(1)} %reshape.556) | copy-start | bytes 9220
  27.3 91.2 %copy-start.55 = (f32[24]{0:T(128)}, f32[24]{0:T(128)S(1)}, u32[]{:S(2)}) copy-start(f32[24]{0:T(128)S(1)} %fusion.116) | copy-start | bytes 292
  27.3 91.2 %copy-start.57 = (f32[24]{0:T(128)}, f32[24]{0:T(128)S(1)}, u32[]{:S(2)}) copy-start(f32[24]{0:T(128)S(1)} %convert_element_type.104) | copy-start | bytes 292
  32.1 63.8 %copy-start.27 = (f32[1792]{0:T(1024)}, f32[1792]{0:T(1024)S(1)}, u32[]{:S(2)}) copy-start(f32[1792]{0:T(1024)S(1)} %get-tuple-element.714) | copy-start | bytes 21508
  32.1 63.8 %copy-start.29 = (f32[1792]{0:T(1024)}, f32[1792]{0:T(1024)S(1)}, u32[]{:S(2)}) copy-start(f32[1792]{0:T(1024)S(1)} %get-tuple-element.715) | copy-start | bytes 21508
  32.1 63.8 %copy-start.31 = (f32[1792]{0:T(1024)}, f32[1792]{0:T(1024)S(1)}, u32[]{:S(2)}) copy-start(f32[1792]{0:T(1024)S(1)} %get-tuple-element.716) | copy-start | bytes 21508
  32.2 63.8 %copy-start.33 = (f32[1792]{0:T(1024)}, f32[1792]{0:T(1024)S(1)}, u32[]{:S(2)}) copy-start(f32[1792]{0:T(1024)S(1)} %get-tuple-element.717) | copy-start | bytes 21508
  33.1 62.9 %copy-start.37 = (f32[1024]{0:T(1024)}, f32[1024]{0:T(1024)S(1)}, u32[]{:S(2)}) copy-start(f32[1024]{0:T(1024)S(1)} %get-tuple-element.829) | copy-start | bytes 12292
  33.1 62.9 %copy-start.39 = (f32[1024]{0:T(1024)}, f32[1024]{0:T(1024)S(1)}, u32[]{:S(2)}) copy-start(f32[1024]{0:T(1024)S(1)} %get-tuple-element.830) | copy-start | bytes 12292
  33.1 62.9 %copy-start.41 = (f32[1024]{0:T(1024)}, f32[1024]{0:T(1024)S(1)}, u32[]{:S(2)}) copy-start(f32[1024]{0:T(1024)S(1)} %get-tuple-element.831) | copy-start | bytes 12292
  40.2 372.1 %copy-start.25 = (f32[1536]{0:T(1024)}, f32[1536]{0:T(1024)S(1)}, u32[]{:S(2)}) copy-start(f32[1536]{0:T(1024)S(1)} %mul.855) | copy-start | bytes 18436
  45.3 367.0 %copy-start.45 = (f32[1536]{0:T(1024)}, f32[1536]{0:T(1024)S(1)}, u32[]{:S(2)}) copy-start(f32[1536]{0:T(1024)S(1)} %reshape.558) | copy-start | bytes 18436
  397.2 15.1 %copy-start.52 = (f32[1024]{0:T(1024)}, f32[1024]{0:T(1024)S(1)}, u32[]{:S(2)}) copy-start(f32[1024]{0:T(1024)S(1)} %fusion.115) | copy-start | bytes 12292
  435.0 594.9 %reduce-scatter.6.cloned.1.call-start = ((), (), s32[]{:S(2)}) async-start(), calls=%async_computation.5 | async-start | bytes 15446016 | tf_op jit(solution)/shard_map/reduce_scatter | solution.py:182
  455.3 12.3 %copy-start.16 = (f32[24,2]{0,1:T(2,128)}, f32[24,2]{0,1:T(2,128)S(1)}, u32[]{:S(2)}) copy-start(f32[24,2]{0,1:T(2,128)S(1)} %slice.252) | copy-start | bytes 580 | tf_op jit(solution)/shard_map/transpose(jvp())/while
  455.5 12.1 copy-start.22
  484.6 52.8 %copy-start.24 = (f32[24]{0:T(128)S(1)}, f32[24]{0:T(128)}, u32[]{:S(2)}) copy-start(f32[24]{0:T(128)} %copy-done.22) | copy-start | bytes 292 | tf_op jit(solution)/shard_map/transpose(jvp())/while
  489.2 50.5 %copy-start.18 = (f32[256,24]{0,1:T(8,128)S(1)}, f32[256,24]{0,1:T(8,128)}, u32[]{:S(2)}) copy-start(f32[256,24]{0,1:T(8,128)} %get-tuple-element.1074) | copy-start | bytes 73732 | tf_op jit(solution)/shard_map/transpose(jvp())/while
  489.2 51.1 %copy-start.36 = (s32[4,256]{1,0:T(4,128)S(1)}, s32[4,256]{1,0:T(4,128)}, u32[]{:S(2)}) copy-start(s32[4,256]{1,0:T(4,128)} %copy-done.35) | copy-start | bytes 12292 | tf_op jit(solution)/shard_map/transpose(jvp())/while
  489.2 51.1 %copy-start.65 = (s32[4]{0:T(128)S(1)}, s32[4]{0:T(128)}, u32[]{:S(2)}) copy-start(s32[4]{0:T(128)} %copy-done.64) | copy-start | bytes 52 | tf_op jit(solution)/shard_map/transpose(jvp())/while
  540.3 11.7 copy-start.35
  540.3 11.7 copy-start.64
  555.0 12.3 %copy-start.16 = (f32[24,2]{0,1:T(2,128)}, f32[24,2]{0,1:T(2,128)S(1)}, u32[]{:S(2)}) copy-start(f32[24,2]{0,1:T(2,128)S(1)} %slice.252) | copy-start | bytes 580 | tf_op jit(solution)/shard_map/transpose(jvp())/while
  555.3 12.1 copy-start.22
  584.3 52.8 %copy-start.24 = (f32[24]{0:T(128)S(1)}, f32[24]{0:T(128)}, u32[]{:S(2)}) copy-start(f32[24]{0:T(128)} %copy-done.22) | copy-start | bytes 292 | tf_op jit(solution)/shard_map/transpose(jvp())/while
  588.9 50.5 %copy-start.18 = (f32[256,24]{0,1:T(8,128)S(1)}, f32[256,24]{0,1:T(8,128)}, u32[]{:S(2)}) copy-start(f32[256,24]{0,1:T(8,128)} %get-tuple-element.1074) | copy-start | bytes 73732 | tf_op jit(solution)/shard_map/transpose(jvp())/while
  588.9 51.1 %copy-start.36 = (s32[4,256]{1,0:T(4,128)S(1)}, s32[4,256]{1,0:T(4,128)}, u32[]{:S(2)}) copy-start(s32[4,256]{1,0:T(4,128)} %copy-done.35) | copy-start | bytes 12292 | tf_op jit(solution)/shard_map/transpose(jvp())/while
  588.9 51.1 %copy-start.65 = (s32[4]{0:T(128)S(1)}, s32[4]{0:T(128)}, u32[]{:S(2)}) copy-start(s32[4]{0:T(128)} %copy-done.64) | copy-start | bytes 52 | tf_op jit(solution)/shard_map/transpose(jvp())/while
  640.0 11.7 copy-start.35
  640.1 11.7 copy-start.64
  654.8 12.3 %copy-start.16 = (f32[24,2]{0,1:T(2,128)}, f32[24,2]{0,1:T(2,128)S(1)}, u32[]{:S(2)}) copy-start(f32[24,2]{0,1:T(2,128)S(1)} %slice.252) | copy-start | bytes 580 | tf_op jit(solution)/shard_map/transpose(jvp())/while
  655.0 12.1 copy-start.22
  684.1 52.8 %copy-start.24 = (f32[24]{0:T(128)S(1)}, f32[24]{0:T(128)}, u32[]{:S(2)}) copy-start(f32[24]{0:T(128)} %copy-done.22) | copy-start | bytes 292 | tf_op jit(solution)/shard_map/transpose(jvp())/while
  688.7 50.5 %copy-start.18 = (f32[256,24]{0,1:T(8,128)S(1)}, f32[256,24]{0,1:T(8,128)}, u32[]{:S(2)}) copy-start(f32[256,24]{0,1:T(8,128)} %get-tuple-element.1074) | copy-start | bytes 73732 | tf_op jit(solution)/shard_map/transpose(jvp())/while
  688.7 51.1 %copy-start.36 = (s32[4,256]{1,0:T(4,128)S(1)}, s32[4,256]{1,0:T(4,128)}, u32[]{:S(2)}) copy-start(s32[4,256]{1,0:T(4,128)} %copy-done.35) | copy-start | bytes 12292 | tf_op jit(solution)/shard_map/transpose(jvp())/while
  688.7 51.1 %copy-start.65 = (s32[4]{0:T(128)S(1)}, s32[4]{0:T(128)}, u32[]{:S(2)}) copy-start(s32[4]{0:T(128)} %copy-done.64) | copy-start | bytes 52 | tf_op jit(solution)/shard_map/transpose(jvp())/while
  739.8 11.7 copy-start.35
  739.8 11.7 copy-start.64
  754.5 12.3 %copy-start.16 = (f32[24,2]{0,1:T(2,128)}, f32[24,2]{0,1:T(2,128)S(1)}, u32[]{:S(2)}) copy-start(f32[24,2]{0,1:T(2,128)S(1)} %slice.252) | copy-start | bytes 580 | tf_op jit(solution)/shard_map/transpose(jvp())/while
  754.8 12.1 copy-start.22
  783.8 52.8 %copy-start.24 = (f32[24]{0:T(128)S(1)}, f32[24]{0:T(128)}, u32[]{:S(2)}) copy-start(f32[24]{0:T(128)} %copy-done.22) | copy-start | bytes 292 | tf_op jit(solution)/shard_map/transpose(jvp())/while
  788.4 50.5 %copy-start.18 = (f32[256,24]{0,1:T(8,128)S(1)}, f32[256,24]{0,1:T(8,128)}, u32[]{:S(2)}) copy-start(f32[256,24]{0,1:T(8,128)} %get-tuple-element.1074) | copy-start | bytes 73732 | tf_op jit(solution)/shard_map/transpose(jvp())/while
  788.4 51.1 %copy-start.36 = (s32[4,256]{1,0:T(4,128)S(1)}, s32[4,256]{1,0:T(4,128)}, u32[]{:S(2)}) copy-start(s32[4,256]{1,0:T(4,128)} %copy-done.35) | copy-start | bytes 12292 | tf_op jit(solution)/shard_map/transpose(jvp())/while
  788.4 51.1 %copy-start.65 = (s32[4]{0:T(128)S(1)}, s32[4]{0:T(128)}, u32[]{:S(2)}) copy-start(s32[4]{0:T(128)} %copy-done.64) | copy-start | bytes 52 | tf_op jit(solution)/shard_map/transpose(jvp())/while
  841.8 12.9 %copy-start.26 = (f32[1536]{0:T(1024)S(1)}, f32[1536]{0:T(1024)}, u32[]{:S(2)}) copy-start(f32[1536]{0:T(1024)} %copy-done.25) | copy-start | bytes 18436
  841.8 21.0 %slice-start = ((s8[7340032]{0:T(1024)(128)(4,1)}), s8[3145728]{0:T(1024)(128)(4,1)S(1)}, s32[]{:S(2)}) async-start(s8[7340032]{0:T(1024)(128)(4,1)} %bitcast.361), calls=%async_computation.9 | async-start | bytes 6291456
  862.8 14.0 %copy-start.30 = (f32[1792]{0:T(1024)S(1)}, f32[1792]{0:T(1024)}, u32[]{:S(2)}) copy-start(f32[1792]{0:T(1024)} %copy-done.29) | copy-start | bytes 21508
  862.8 14.0 %copy-start.32 = (f32[1792]{0:T(1024)S(1)}, f32[1792]{0:T(1024)}, u32[]{:S(2)}) copy-start(f32[1792]{0:T(1024)} %copy-done.31) | copy-start | bytes 21508
  862.8 14.0 %copy-start.34 = (f32[1792]{0:T(1024)S(1)}, f32[1792]{0:T(1024)}, u32[]{:S(2)}) copy-start(f32[1792]{0:T(1024)} %copy-done.33) | copy-start | bytes 21508
  909.0 152.9 %reduce-scatter.10.cloned.1.call-start = ((), (), s32[]{:S(2)}) async-start(), calls=%async_computation.7 | async-start | bytes 1376256
  910.4 304.0 %all-reduce.36.cloned.1.call-start = ((), (), s32[]{:S(2)}) async-start(), calls=%async_computation.8 | async-start | bytes 15015936 | tf_op jit(solution)/shard_map/psum | solution.py:191
  1029.9 12.4 %copy-start.47 = (f32[1536]{0:T(1024)S(1)}, f32[1536]{0:T(1024)}, u32[]{:S(2)}) copy-start(f32[1536]{0:T(1024)} %get-tuple-element.796) | copy-start | bytes 18436
  1029.9 12.6 %copy-start.60 = (f32[24]{0:T(128)S(1)}, f32[24]{0:T(128)}, u32[]{:S(2)}) copy-start(f32[24]{0:T(128)} %get-tuple-element.828) | copy-start | bytes 292
  1029.9 12.6 %copy-start.63 = (bf16[24]{0:T(256)(128)(2,1)S(1)}, bf16[24]{0:T(256)(128)(2,1)}, u32[]{:S(2)}) copy-start(bf16[24]{0:T(256)(128)(2,1)} %copy-done.62) | copy-start | bytes 148
  1029.9 12.6 %copy-start.54 = (f32[1536]{0:T(1024)S(1)}, f32[1536]{0:T(1024)}, u32[]{:S(2)}) copy-start(f32[1536]{0:T(1024)} %get-tuple-element.708) | copy-start | bytes 18436
  1029.9 12.6 %copy-start.59 = (f32[24]{0:T(128)S(1)}, f32[24]{0:T(128)}, u32[]{:S(2)}) copy-start(f32[24]{0:T(128)} %get-tuple-element.798) | copy-start | bytes 292
  1029.9 20.8 %copy-start.44 = (f32[1024]{0:T(1024)S(1)}, f32[1024]{0:T(1024)}, u32[]{:S(2)}) copy-start(f32[1024]{0:T(1024)} %copy-done.43) | copy-start | bytes 12292
  1029.9 20.8 %copy-start.13 = (bf16[1024,768]{1,0:T(8,128)(2,1)S(1)}, bf16[1024,768]{1,0:T(8,128)(2,1)}, u32[]{:S(2)}) copy-start(bf16[1024,768]{1,0:T(8,128)(2,1)} %param.18) | copy-start | bytes 4718596
  1042.3 12.7 %copy-start.46 = (f32[1536]{0:T(1024)S(1)}, f32[1536]{0:T(1024)}, u32[]{:S(2)}) copy-start(f32[1536]{0:T(1024)} %copy-done.45) | copy-start | bytes 18436
  1042.3 12.7 %copy-start.53 = (f32[1024]{0:T(1024)S(1)}, f32[1024]{0:T(1024)}, u32[]{:S(2)}) copy-start(f32[1024]{0:T(1024)} %copy-done.52) | copy-start | bytes 12292
  (58 other events, 521.5 us)
Sparse Core Ops, SparseCore 0:
  9.6 70.5 all-gather.5
  81.7 36.0 all-gather.7
  435.1 60.3 reduce-scatter.7
  909.1 120.7 reduce-scatter.5
  1032.6 19.4 reduce-scatter.9
  1055.8 158.6 all-reduce.35
where the time goes:
time: 1250 us; the launch traced here: 1230 us
  local copies, waits for them, and re-layouts  467 us (37%)
  matrix products  258 us (21%)
  waiting for transfers between devices  237 us (19%)
  other arithmetic  141 us (11%)
  blocking collectives  94.9 us (8%)
  between operations  18.4 us (1%)
  loops' own time  12.5 us (1%)
    dynamic_update_slice x28, local copies, waits for them, and re-layouts, state_scan(): ending, outputs = lax.scan(jax.checkpoint(block_step), start, inputs)  341 us
    reduce_scatter x1, waiting for transfers between devices, body(): lax.psum_scatter(gradients[1], 'shard', scatter_dimension=0, tiled=True)  117 us
    dot_general x12, matrix products, block_step(): jnp.einsum('hts,shp->thp', kernel * pair_scores[None], weighted, precisio...  107 us
    psum x1, waiting for transfers between devices, body(): lax.psum((grouped[0], grouped[1], grouped[2], grouped[3], grouped[4], gro...  84 us
    psum x1, blocking collectives, body(): lax.psum((grouped[0], grouped[1], grouped[2], grouped[3], grouped[4], gro...  63.4 us
    dot_general x16, matrix products, block_step(): jnp.einsum('tn,hpn->thp', c_rows, hidden, precision=highest)  36.7 us
    all_gather x1, waiting for transfers between devices, body(): lax.all_gather(shards[1], 'shard', axis=0, tiled=True)  34.8 us
    dot_general x12, matrix products, block_step(): jnp.einsum('shp,sn->hpn', weighted * leaving.T[:, :, None], b_rows, preci...  32.4 us
  transfers between devices with their start and end apart: 6, of which 3 were waited for; matrix products, arithmetic and copies ran while one was open for 67% of the time, Pallas kernels for 0%

commit v1 on v0

v1 whole, which is shorter than its diff:
```python
import functools

import jax
import jax.numpy as jnp
from jax import lax
from jax.experimental import pallas as pl
from jax.experimental.pallas import tpu as pltpu
from jax.sharding import PartitionSpec as P

HEADS = 24
HEADDIM = 64
STATE = 128
CONV = 4
BLOCK = 128
INNER = 1536
XBC = 1792
WIDE = INNER + XBC
LANES = 128

eps = 1e-05
highest = lax.Precision.HIGHEST
f32 = jnp.float32
bf16 = jnp.bfloat16


def mm(a, b, contract=((1,), (0,))):
    return lax.dot_general(a, b, (contract, ((), ())), preferred_element_type=f32)


def sigmoid(v):
    return 1.0 / (1.0 + jnp.exp(-v))


def softplus(v):
    small = jnp.exp(-jnp.abs(v))
    series = small * (1.0 - small * (0.5 - small * (1.0 / 3.0 - small * 0.25)))
    return jnp.maximum(v, 0.0) + jnp.where(small < 0.03, series, jnp.log(1.0 + small))


def spread(per_head, spread_mat):
    high = per_head.astype(bf16)
    rest = (per_head - high.astype(f32)).astype(bf16)
    return mm(jnp.concatenate([high, rest], axis=1), spread_mat)


def head_sum(per_channel, spread_mat):
    high = per_channel.astype(bf16)
    rest = (per_channel - high.astype(f32)).astype(bf16)
    one = spread_mat[:LANES, :]
    return mm(high, one, ((1,), (1,))) + mm(rest, one, ((1,), (1,)))


def block_terms(raw, aux, seg_row, head_vecs):
    length = raw.shape[0]
    pre = raw + head_vecs[0:1, :]
    step = softplus(pre)
    rate = -jnp.exp(head_vecs[1:2, :])
    decay = rate * step
    row = lax.broadcasted_iota(jnp.int32, (length, length), 0)
    col = lax.broadcasted_iota(jnp.int32, (length, length), 1)
    lower = (row >= col).astype(f32)
    running = lax.dot_general(
        lower, decay, (((1,), (0,)), ((), ())), precision=highest, preferred_element_type=f32
    )
    allowed = (row >= col) & (aux[:, 5:6] == seg_row)
    entering = jnp.exp(running) * aux[:, 3:4]
    leaving = jnp.exp(running[length - 1 : length, :] - running) * aux[:, 4:5]
    return pre, step, rate, decay, running, allowed, entering, leaving, lower


def lane_pair(values, first):
    lane = lax.broadcasted_iota(jnp.int32, values.shape, 1)
    zero = jnp.zeros_like(values)
    return jnp.concatenate(
        [jnp.where(lane < HEADDIM, values, zero), jnp.where(lane >= HEADDIM, values, zero)], axis=0
    )


def spread_of(running, running_t, head):
    diff = running[:, head : head + 1] - running_t[head : head + 1, :]
    return jnp.exp(jnp.minimum(diff, 0.0))


def forward_kernel(
    u_ref, aux_ref, seg_ref, gain_ref, in_ref, step_ref, conv_w_ref, conv_b_ref, head_ref, skip_ref,
    gate_gain_ref, out_w_ref, spread_ref,
    normed_ref, gate_ref, ci_ref, conv_ref, raw_ref, y_ref, state_ref, mixed_ref, out_ref,
    buf, hidden, y_buf,
):
    @pl.when(pl.program_id(0) == 0)
    def _():
        buf[0:8, :] = jnp.zeros((8, XBC), f32)
        hidden[...] = jnp.zeros_like(hidden)

    u = u_ref[...].astype(f32)
    inv = lax.rsqrt(jnp.mean(u * u, axis=-1, keepdims=True) + eps)
    normed = (u * inv * gain_ref[...]).astype(bf16)
    normed_ref[...] = normed
    gate = mm(normed, in_ref[:, :INNER])
    gate_ref[...] = gate
    conv_in = mm(normed, in_ref[:, INNER:WIDE])
    raw = mm(normed, step_ref[...])
    raw_ref[...] = raw
    ci_ref[...] = conv_in.astype(bf16)
    aux = aux_ref[...]
    buf[8 : 8 + BLOCK, :] = conv_in
    conv = conv_b_ref[...] + conv_w_ref[3:4, :] * conv_in
    for k in range(1, CONV):
        conv = conv + conv_w_ref[3 - k : 4 - k, :] * buf[8 - k : 8 - k + BLOCK, :] * aux[:, k - 1 : k]
    buf[0:8, :] = conv_in[BLOCK - 8 :, :]
    conv_ref[...] = conv
    active = conv * sigmoid(conv)
    values = active[:, :INNER]
    b_low = active[:, INNER : INNER + STATE].astype(bf16)
    c_low = active[:, INNER + STATE :].astype(bf16)
    _, step, _, _, running, allowed, entering, leaving, _ = block_terms(
        raw, aux, seg_ref[0], head_ref[...]
    )
    running_t = jnp.transpose(running)
    spread_mat = spread_ref[...]
    weighted = values * spread(step, spread_mat)
    w_low = weighted.astype(bf16)
    scores = jnp.where(allowed, mm(c_low, b_low, ((1,), (1,))), 0.0)
    enter_wide = spread(entering, spread_mat)
    leave_wide = spread(leaving, spread_mat)
    for pair in range(HEADS // 2):
        cols = slice(pair * LANES, (pair + 1) * LANES)
        first = (spread_of(running, running_t, 2 * pair) * scores).astype(bf16)
        second = (spread_of(running, running_t, 2 * pair + 1) * scores).astype(bf16)
        y_buf[:, cols] = mm(
            jnp.concatenate([first, second], axis=1), lane_pair(w_low[:, cols], pair)
        )
    state = hidden[...]
    state_low = state.astype(bf16)
    state_ref[0] = state_low
    y = y_buf[...] + mm(c_low, state_low) * enter_wide + skip_ref[...] * values
    hidden[...] = state * enter_wide[BLOCK - 1 :, :] + mm(
        b_low, (weighted * leave_wide).astype(bf16), ((0,), (0,))
    )
    y_ref[...] = y
    gated = y * (gate * sigmoid(gate))
    inv_g = lax.rsqrt(jnp.mean(gated * gated, axis=-1, keepdims=True) + eps)
    mixed = (gated * inv_g * gate_gain_ref[...]).astype(bf16)
    mixed_ref[...] = mixed
    out_ref[...] = (u + mm(mixed, out_w_ref[...])).astype(bf16)


def backward_kernel(
    u_ref, g_ref, aux_ref, seg_ref, gain_ref, in_ref, step_ref, conv_w_ref, head_ref, skip_ref,
    gate_gain_ref, out_w_ref, spread_ref, gate_ref, ci_ref, conv_ref, raw_ref, y_ref, state_ref,
    ingrad_ref, zx_ref, rawg_ref, dgain_ref, dconv_w_ref, dconv_b_ref, dhead_ref, dskip_ref,
    dgate_gain_ref,
    buf, d_hidden, dw_buf,
):
    @pl.when(pl.program_id(0) == 0)
    def _():
        buf[BLOCK:, :] = jnp.zeros((8, XBC), f32)
        d_hidden[...] = jnp.zeros_like(d_hidden)
        for ref in (dgain_ref, dconv_w_ref, dconv_b_ref, dhead_ref, dskip_ref, dgate_gain_ref):
            ref[...] = jnp.zeros_like(ref)

    def total(v):
        return jnp.sum(v, axis=0, keepdims=True)

    g = g_ref[...]
    aux = aux_ref[...]
    spread_mat = spread_ref[...]
    mixed_grad = mm(g, out_w_ref[...], ((1,), (1,)))
    gate = gate_ref[...]
    y = y_ref[...]
    gate_sig = sigmoid(gate)
    gate_act = gate * gate_sig
    gated = y * gate_act
    inv_g = lax.rsqrt(jnp.mean(gated * gated, axis=-1, keepdims=True) + eps)
    dgate_gain_ref[...] += total(mixed_grad * gated * inv_g)
    scaled = mixed_grad * gate_gain_ref[...]
    mean_term = jnp.mean(scaled * gated, axis=-1, keepdims=True)
    d_gated = inv_g * scaled - gated * (inv_g * inv_g * inv_g * mean_term)
    dy = d_gated * gate_act
    zx_ref[:, :INNER] = (d_gated * y * (gate_sig * (1.0 + gate * (1.0 - gate_sig)))).astype(bf16)

    conv = conv_ref[...]
    conv_sig = sigmoid(conv)
    active = conv * conv_sig
    slope = conv_sig * (1.0 + conv * (1.0 - conv_sig))
    values = active[:, :INNER]
    b_low = active[:, INNER : INNER + STATE].astype(bf16)
    c_low = active[:, INNER + STATE :].astype(bf16)
    pre, step, rate, decay, running, allowed, entering, leaving, lower = block_terms(
        raw_ref[...], aux, seg_ref[0], head_ref[...]
    )
    running_t = jnp.transpose(running)
    step_wide = spread(step, spread_mat)
    weighted = values * step_wide
    w_low = weighted.astype(bf16)
    scores = jnp.where(allowed, mm(c_low, b_low, ((1,), (1,))), 0.0)
    enter_wide = spread(entering, spread_mat)
    leave_wide = spread(leaving, spread_mat)
    dskip_ref[...] += total(dy * values)
    dy_low = dy.astype(bf16)
    d_scores = jnp.zeros((BLOCK, BLOCK), f32)
    d_running = jnp.zeros((BLOCK, LANES), f32)
    half = lax.broadcasted_iota(jnp.int32, (2 * BLOCK, LANES), 0) // BLOCK
    lane = lax.broadcasted_iota(jnp.int32, (2 * BLOCK, LANES), 1)
    for pair in range(HEADS // 2):
        cols = slice(pair * LANES, (pair + 1) * LANES)
        dy_two = lane_pair(dy_low[:, cols], pair)
        d_kernel = mm(dy_two, w_low[:, cols], ((1,), (1,)))
        spread_a = spread_of(running, running_t, 2 * pair)
        spread_b = spread_of(running, running_t, 2 * pair + 1)
        part_a = d_kernel[:BLOCK] * spread_a
        part_b = d_kernel[BLOCK:] * spread_b
        d_scores = d_scores + (part_a + part_b)
        kernel_two = jnp.concatenate(
            [(spread_a * scores).astype(bf16), (spread_b * scores).astype(bf16)], axis=0
        )
        dw_buf[:, cols] = mm(kernel_two, dy_two, ((0,), (0,)))
        flow_a = (part_a * scores).astype(bf16)
        flow_b = (part_b * scores).astype(bf16)
        marks = jnp.where(lane == 2 * pair + half, 1.0, 0.0).astype(bf16)
        d_running = d_running + (
            mm(jnp.concatenate([flow_a, flow_b], axis=1), marks)
            - mm(jnp.concatenate([flow_a, flow_b], axis=0), marks, ((0,), (0,)))
        )
    state_low = state_ref[0]
    d_state = d_hidden[...]
    d_state_low = d_state.astype(bf16)
    entered = dy * enter_wide
    entered_low = entered.astype(bf16)
    d_running = d_running + head_sum(entered * mm(c_low, state_low), spread_mat)
    left = weighted * leave_wide
    left_low = left.astype(bf16)
    d_left = mm(b_low, d_state_low)
    left_flow = head_sum(left * d_left, spread_mat)
    d_running = d_running - left_flow
    carried = enter_wide[BLOCK - 1 :, :]
    carry_row = total(d_state * state_low.astype(f32)) * carried
    carry_flow = head_sum(jnp.broadcast_to(carry_row, (8, INNER)), spread_mat)[0:1, :]
    d_hidden[...] = d_state * carried + mm(c_low, entered_low, ((0,), (0,)))
    d_weighted = dw_buf[...] + d_left * leave_wide
    d_decay = (
        lax.dot_general(
            lower, d_running, (((0,), (0,)), ((), ())), precision=highest, preferred_element_type=f32
        )
        + total(left_flow)
        + carry_flow
    )
    d_step = d_decay * rate + head_sum(d_weighted * values, spread_mat)
    d_raw = d_step * sigmoid(pre)
    dhead_ref[0:1, :] += total(d_raw)
    dhead_ref[1:2, :] += total(d_decay * decay)
    raw_low = d_raw.astype(bf16)
    rawg_ref[...] = raw_low
    d_scores_low = jnp.where(allowed, d_scores, 0.0).astype(bf16)
    d_c = mm(entered_low, state_low, ((1,), (1,))) + mm(d_scores_low, b_low)
    d_b = mm(left_low, d_state_low, ((1,), (1,))) + mm(d_scores_low, c_low, ((0,), (0,)))
    buf[:BLOCK, :INNER] = (dy * skip_ref[...] + d_weighted * step_wide) * slope[:, :INNER]
    buf[:BLOCK, INNER : INNER + STATE] = d_b * slope[:, INNER : INNER + STATE]
    buf[:BLOCK, INNER + STATE :] = d_c * slope[:, INNER + STATE :]
    conv_in = ci_ref[...].astype(f32)
    d_conv = buf[:BLOCK, :]
    dconv_b_ref[...] += total(d_conv)
    dconv_w_ref[3:4, :] += total(conv_in * d_conv)
    d_in = conv_w_ref[3:4, :] * d_conv
    for k in range(1, CONV):
        later = buf[k : BLOCK + k, :] * aux[:, 5 + k : 6 + k]
        d_in = d_in + conv_w_ref[3 - k : 4 - k, :] * later
        dconv_w_ref[3 - k : 4 - k, :] += total(conv_in * later)
    buf[BLOCK:, :] = d_conv[:8, :]
    zx_ref[:, INNER:] = d_in.astype(bf16)
    normed_grad = mm(zx_ref[...], in_ref[:, :WIDE], ((1,), (1,))) + mm(
        raw_low, step_ref[...], ((1,), (1,))
    )
    u = u_ref[...].astype(f32)
    inv = lax.rsqrt(jnp.mean(u * u, axis=-1, keepdims=True) + eps)
    dgain_ref[...] += total(normed_grad * u * inv)
    lifted = normed_grad * gain_ref[...]
    mean_u = jnp.mean(lifted * u, axis=-1, keepdims=True)
    ingrad_ref[...] = (
        g.astype(f32) + inv * lifted - u * (inv * inv * inv * mean_u)
    ).astype(bf16)


def layer(layer_in, segment, cotangent, gain, w_in, conv_w, conv_b, dt_bias, a_log, skip, gate_gain, w_out):
    tokens, width = layer_in.shape
    blocks = tokens // BLOCK
    proj = w_in.shape[1]
    shifted = [jnp.pad(segment, (k, 0), constant_values=-1)[:tokens] for k in range(CONV)]
    after = [jnp.pad(segment, (0, k), constant_values=-1)[k:] for k in range(CONV)]
    by_block = segment.reshape(blocks, BLOCK)
    before = jnp.concatenate([jnp.full((1,), -1, segment.dtype), by_block[:-1, -1]])
    aux = jnp.stack(
        [shifted[k] == segment for k in (1, 2, 3)]
        + [
            (by_block == before[:, None]).reshape(tokens),
            (by_block == by_block[:, -1:]).reshape(tokens),
            segment,
        ]
        + [after[k] == segment for k in (1, 2, 3)]
        + [segment] * 7,
        axis=1,
    ).astype(f32)
    seg_rows = segment.astype(f32).reshape(blocks, 1, BLOCK)
    w_step = jnp.pad(w_in[:, WIDE:], ((0, 0), (0, LANES - HEADS)))
    pad_head = lambda v: jnp.pad(v.astype(f32), (0, LANES - HEADS))
    heads = jnp.stack([pad_head(dt_bias), pad_head(a_log)] + [jnp.zeros((LANES,), f32)] * 6)
    skip_wide = jnp.repeat(skip.astype(f32), HEADDIM).reshape(1, INNER)
    owner = jnp.arange(INNER) // HEADDIM
    one = (jnp.arange(LANES)[:, None] == owner[None, :]).astype(bf16)
    spread_mat = jnp.concatenate([one, one], axis=0)
    gain_row = gain.astype(f32).reshape(1, width)
    conv_w = conv_w.astype(f32)
    conv_b = conv_b.astype(f32).reshape(1, XBC)
    gate_row = gate_gain.astype(f32).reshape(1, INNER)

    def full(a):
        return pl.BlockSpec(a.shape, lambda i: (0,) * a.ndim, pipeline_mode=pl.Buffered(1))

    def rows(cols, order):
        return pl.BlockSpec((BLOCK, cols), lambda i: (order(i), 0))

    fwd = lambda i: i
    bwd = lambda i: blocks - 1 - i
    shape = jax.ShapeDtypeStruct
    params = pltpu.CompilerParams(
        dimension_semantics=("arbitrary",), vmem_limit_bytes=60 * 1024 * 1024
    )
    normed, gate, conv_in, conv, raw, y, states, mixed, layer_out = pl.pallas_call(
        forward_kernel,
        grid=(blocks,),
        in_specs=[
            rows(width, fwd), rows(16, fwd), pl.BlockSpec((1, 1, BLOCK), lambda i: (i, 0, 0)),
            full(gain_row), full(w_in), full(w_step), full(conv_w), full(conv_b), full(heads),
            full(skip_wide), full(gate_row), full(w_out), full(spread_mat),
        ],
        out_specs=[
            rows(width, fwd), rows(INNER, fwd), rows(XBC, fwd), rows(XBC, fwd), rows(LANES, fwd),
            rows(INNER, fwd), pl.BlockSpec((1, STATE, INNER), lambda i: (i, 0, 0)),
            rows(INNER, fwd), rows(width, fwd),
        ],
        out_shape=[
            shape((tokens, width), bf16), shape((tokens, INNER), f32), shape((tokens, XBC), bf16),
            shape((tokens, XBC), f32), shape((tokens, LANES), f32), shape((tokens, INNER), f32),
            shape((blocks, STATE, INNER), bf16), shape((tokens, INNER), bf16),
            shape((tokens, width), bf16),
        ],
        scratch_shapes=[
            pltpu.VMEM((BLOCK + 8, XBC), f32), pltpu.VMEM((STATE, INNER), f32),
            pltpu.VMEM((BLOCK, INNER), f32),
        ],
        compiler_params=params,
        cost_estimate=pl.CostEstimate(
            flops=2 * tokens * width * (proj + INNER) * 2, bytes_accessed=40_000_000,
            transcendentals=tokens * 8000,
        ),
        name="layer_forward",
    )(layer_in, aux, seg_rows, gain_row, w_in, w_step, conv_w, conv_b, heads, skip_wide, gate_row,
      w_out, spread_mat)
    acc = lambda r, c: pl.BlockSpec((r, c), lambda i: (0, 0))
    input_grad, zx_grad, raw_grad, d_gain, d_conv_w, d_conv_b, d_heads, d_skip, d_gate_gain = (
        pl.pallas_call(
            backward_kernel,
            grid=(blocks,),
            in_specs=[
                rows(width, bwd), rows(width, bwd), rows(16, bwd),
                pl.BlockSpec((1, 1, BLOCK), lambda i: (blocks - 1 - i, 0, 0)),
                full(gain_row), full(w_in), full(w_step), full(conv_w), full(heads),
                full(skip_wide), full(gate_row), full(w_out), full(spread_mat),
                rows(INNER, bwd), rows(XBC, bwd), rows(XBC, bwd), rows(LANES, bwd),
                rows(INNER, bwd),
                pl.BlockSpec((1, STATE, INNER), lambda i: (blocks - 1 - i, 0, 0)),
            ],
            out_specs=[
                rows(width, bwd), rows(WIDE, bwd), rows(LANES, bwd), acc(1, width), acc(CONV, XBC),
                acc(1, XBC), acc(8, LANES), acc(1, INNER), acc(1, INNER),
            ],
            out_shape=[
                shape((tokens, width), bf16), shape((tokens, WIDE), bf16),
                shape((tokens, LANES), bf16), shape((1, width), f32), shape((CONV, XBC), f32),
                shape((1, XBC), f32), shape((8, LANES), f32), shape((1, INNER), f32),
                shape((1, INNER), f32),
            ],
            scratch_shapes=[
                pltpu.VMEM((BLOCK + 8, XBC), f32), pltpu.VMEM((STATE, INNER), f32),
                pltpu.VMEM((BLOCK, INNER), f32),
            ],
            compiler_params=params,
            cost_estimate=pl.CostEstimate(
                flops=2 * tokens * width * (proj + INNER) * 3, bytes_accessed=40_000_000,
                transcendentals=tokens * 8000,
            ),
            name="layer_backward",
        )(layer_in, cotangent, aux, seg_rows, gain_row, w_in, w_step, conv_w, heads, skip_wide,
          gate_row, w_out, spread_mat, gate, conv_in, conv, raw, y, states)
    )
    small = (
        d_gain.reshape(width), d_conv_w, d_conv_b.reshape(XBC), d_heads[0, :HEADS],
        d_heads[1, :HEADS], d_skip.reshape(HEADS, HEADDIM).sum(axis=1), d_gate_gain.reshape(INNER),
    )
    return layer_out, input_grad, normed, mixed, zx_grad, raw_grad, small


def own(full, axis):
    count = lax.axis_size("shard")
    size = full.shape[axis] // count
    return lax.dynamic_slice_in_dim(full, lax.axis_index("shard") * size, size, axis)


def body(
    layer_in, segment_ids, cotangent, norm_gain, in_weight, conv_weight, conv_bias, dt_bias, a_log,
    skip_gain, gate_gain, out_weight,
):
    vectors = (norm_gain, conv_weight, conv_bias, dt_bias, a_log, skip_gain, gate_gain)
    packed = jnp.concatenate([v.reshape(-1) for v in vectors])
    packed = lax.all_gather(packed, "shard", axis=0)
    w_in = lax.all_gather(in_weight, "shard", axis=0, tiled=True)
    w_out = lax.all_gather(out_weight, "shard", axis=0, tiled=True)
    whole, at = [], 0
    for v in vectors:
        piece = packed[:, at : at + v.size]
        at += v.size
        if v.ndim == 2:
            piece = piece.reshape((-1,) + v.shape).transpose(1, 0, 2).reshape(v.shape[0], -1)
        else:
            piece = piece.reshape(-1)
        whole.append(piece)
    gain, conv_w, conv_b, step_bias, alog, skip, gate_vec = whole
    layer_out, input_grad, normed, mixed, zx_grad, raw_grad, small = layer(
        layer_in, segment_ids.reshape(-1), cotangent, gain, w_in, conv_w, conv_b, step_bias, alog,
        skip, gate_vec, w_out,
    )
    both = ("shard", "rep")
    factor = 1.0 / (lax.axis_size("shard") * lax.axis_size("rep"))
    out_grad = jnp.einsum("ti,td->id", mixed, cotangent, preferred_element_type=f32).astype(bf16)
    out_sum = lax.psum(lax.psum_scatter(out_grad, "shard", scatter_dimension=0, tiled=True), "rep")
    in_grad = jnp.concatenate(
        [
            jnp.einsum("td,tp->dp", normed, zx_grad, preferred_element_type=f32),
            jnp.einsum("td,tp->dp", normed, raw_grad[:, :HEADS], preferred_element_type=f32),
        ],
        axis=1,
    ).astype(bf16)
    in_sum = lax.psum(lax.psum_scatter(in_grad, "shard", scatter_dimension=0, tiled=True), "rep")
    flat = lax.psum(jnp.concatenate([v.reshape(-1) for v in small]), both) * factor
    outs, at = [], 0
    for v in small:
        piece = flat[at : at + v.size].reshape(v.shape)
        at += v.size
        outs.append(own(piece, v.ndim - 1))
    return (
        layer_out, input_grad, outs[0], in_sum.astype(f32) * factor, outs[1], outs[2], outs[3],
        outs[4], outs[5], outs[6], out_sum.astype(f32) * factor,
    )


def solution(mesh):
    in_specs = (
        P(("shard", "rep"), None),
        P(("shard", "rep"), None),
        P(("shard", "rep"), None),
        P("shard"),
        P("shard", None),
        P(None, "shard"),
        P("shard"),
        P("shard"),
        P("shard"),
        P("shard"),
        P("shard"),
        P("shard", None),
    )
    out_specs = (
        P(("shard", "rep"), None),
        P(("shard", "rep"), None),
        P("shard"),
        P("shard", None),
        P(None, "shard"),
        P("shard"),
        P("shard"),
        P("shard"),
        P("shard"),
        P("shard"),
        P("shard", None),
    )
    return jax.shard_map(body, mesh=mesh, in_specs=in_specs, out_specs=out_specs, check_vma=False)
```

time: 1250 us -> 451 us (0.36); the launches traced: 1230 us -> 450 us
  local copies, waits for them, and re-layouts: 467 us -> 23.3 us
  matrix products: 258 us -> 16 us
  other arithmetic: 141 us -> 12.4 us
  Pallas kernels: 0 us -> 111 us
  blocking collectives: 94.9 us -> 50.5 us
  waiting for transfers between devices: 237 us -> 222 us
  loops' own time: 12.5 us -> 0 us
    dynamic_update_slice x28 -> x0, local copies, waits for them, and re-layouts: 341 us -> none  [state_scan(): ending, outputs = lax.scan(jax.checkpoint(block_step), start, inputs)]
    dot_general x62 -> x3, matrix products: 258 us -> 16 us  [the longest x1 8.7 us: body(): jnp.einsum('td,tp->dp', normed, zx_grad, preferred_element_type=f32)]
    pallas_call x0 -> x2, Pallas kernels: none -> 111 us  [the longest x1 77.9 us: layer(): pl.pallas_call(backward_kernel, grid=(blocks,), in_specs=[rows(width, bwd...]
    all_gather x2, waiting for transfers between devices: 34.8 us -> 87.8 us  [the longest x1 51.8 us: body(): w_in = lax.all_gather(in_weight, 'shard', axis=0, tiled=True)]
    reduce_scatter x2, waiting for transfers between devices: 117 us -> 66.4 us  [the longest x1 66.4 us: body(): lax.psum_scatter(in_grad, 'shard', scatter_dimension=0, tiled=True)]
    reduce_sum x14 -> x1, other arithmetic: 44.3 us -> 0.12 us  [layer(): d_skip.reshape(HEADS, HEADDIM).sum(axis=1)]
    mul x41 -> x3, other arithmetic: 37.6 us -> 5.98 us  [the longest x1 4.41 us: body(): in_sum.astype(f32) * factor]
    reshape x14 -> x4, local copies, waits for them, and re-layouts: 23 us -> 0.12 us  [the longest x1 0.07 us: layer(): d_skip.reshape(HEADS, HEADDIM).sum(axis=1)]
  transfers between devices with their start and end apart: 6 -> 5, of which waited for: 3 -> 4; matrix products, arithmetic and copies ran while one was open for 67% -> 6% of each run, Pallas kernels for 0% -> 17%
where the time goes in v1:
time: 451 us; the launch traced here: 450 us
  waiting for transfers between devices  222 us (49%)
  Pallas kernels  111 us (25%)
  blocking collectives  50.5 us (11%)
  local copies, waits for them, and re-layouts  23.3 us (5%)
  matrix products  16 us (4%)
  between operations  14.8 us (3%)
  other arithmetic  12.4 us (3%)
    pallas_call x1, Pallas kernels, layer(): pl.pallas_call(backward_kernel, grid=(blocks,), in_specs=[rows(width, bwd...  77.9 us
    psum x1, waiting for transfers between devices, body(): lax.psum(lax.psum_scatter(in_grad, 'shard', scatter_dimension=0, tiled=Tr...  66.8 us
    reduce_scatter x1, waiting for transfers between devices, body(): lax.psum_scatter(in_grad, 'shard', scatter_dimension=0, tiled=True)  66.4 us
    all_gather x1, waiting for transfers between devices, body(): w_in = lax.all_gather(in_weight, 'shard', axis=0, tiled=True)  51.8 us
    psum x1, blocking collectives, body(): lax.psum(jnp.concatenate([v.reshape(-1) for v in small]), both) * factor  40.7 us
    all_gather x1, waiting for transfers between devices, body(): w_out = lax.all_gather(out_weight, 'shard', axis=0, tiled=True)  36 us
    pallas_call x1, Pallas kernels, layer(): pl.pallas_call(forward_kernel, grid=(blocks,), in_specs=[rows(width, fwd)...  33.3 us
    unnamed x45, local copies, waits for them, and re-layouts  14.1 us
  transfers between devices with their start and end apart: 5, of which 4 were waited for; matrix products, arithmetic and copies ran while one was open for 6% of the time, Pallas kernels for 17%

profile of v1, /device:TPU:0, one launch (start us, length us, event | category | flops | bytes accessed | tf_op | source)
XLA Modules:
  0.0 450.3 jit_solution(3941535657037275698)
XLA Ops:
  7.2 4.4 copy.63
  11.8 0.7 all-gather.6.cloned.1.call-update
  12.5 0.1 slice.81
  12.6 0.1 slice.82
  12.7 0.1 fusion.10
  12.8 0.1 copy.67
  12.8 0.1 copy.68
  13.0 0.6 dynamic-slice
  14.3 0.1 concatenate.19
  14.4 0.4 dynamic-update-slice
  14.7 9.8 %all-reduce.9 = bf16[11336]{0:T(1024)(128)(2,1)S(1)} all-reduce(bf16[11336]{0:T(1024)(128)(2,1)S(1)} %dynamic-update-slice), channel_id=2, replica_groups=mesh['shard'=2,'rep'=16] {'shard'}, use_global_device_ids=true, to_apply=%add.9 | all-reduce | flops 11336 | bytes 45344
  24.5 0.1 reshape.197
  24.7 0.1 pad_add_fusion
  24.7 0.1 eq.78
  24.9 0.1 slice_convert_fusion
  25.0 0.1 stack.74
  25.1 0.2 copy.62
  25.3 0.9 convert_element_type.122.aux_ref
  26.2 0.1 convert_element_type.133
  26.2 0.1 convert_element_type.134
  26.3 0.1 pad.52.clone
  26.4 0.1 pad.53.clone
  26.5 0.1 reshape.194
  26.6 0.1 broadcast_in_dim.2
  26.6 0.7 reshape_reshape.10.skip_ref
  27.3 0.6 copy.70
  27.9 0.1 convert_bitcast_fusion.2
  28.0 0.6 copy.72
  28.6 0.6 copy.69
  29.2 0.6 copy.71
  29.8 0.7 maximum_maximum_fusion.head_ref
  30.5 0.6 convert_bitcast_fusion.3.seg_ref
  31.1 0.1 iota_compare_fusion
  31.2 0.9 add_convert_fusion.spread_ref
  32.1 51.8 %all-gather.4.cloned.1.call-done.in_ref = bf16[768,3352]{1,0:T(8,128)(2,1)} async-done(((bf16[384,3352]{1,0:T(8,128)(2,1)}), bf16[768,3352]{1,0:T(8,128)(2,1)}) %all-gather.4.cloned.1.call-update) | async-done | bytes 5148688 | tf_op jit(solution)/shard_map/all_gather | solution.py:416
  83.9 0.9 slice.105
  84.9 0.7 pad.43.step_ref
  85.6 36.0 %all-gather.6.cloned.1.call-done.out_w_ref = bf16[1536,768]{1,0:T(8,128)(2,1)} async-done(((bf16[768,768]{1,0:T(8,128)(2,1)}), bf16[1536,768]{1,0:T(8,128)(2,1)}) %all-gather.6.cloned.1.call-update) | async-done | bytes 2359312 | tf_op jit(solution)/shard_map/all_gather | solution.py:417
  121.6 33.3 %layer_forward.1 = (bf16[1024,768]{1,0:T(8,128)(2,1)}, f32[1024,1536]{1,0:T(8,128)}, bf16[1024,1792]{1,0:T(8,128)(2,1)}, f32[1024,1792]{1,0:T(8,128)}, f32[1024,...) custom-call(bf16[1024,768]{1,0:T(8,128)(2,1)} %u_ref.3, ...), custom_call_target="tpu_custom_call" | custom-call | flops 15376318464 | bytes 40000000 | tf_op jit(solution)/shard_map/layer_forward/pallas_call | solution.py:328
  154.9 6.0 %convolution_convert_fusion.1 = bf16[1536,768]{1,0:T(8,128)(2,1)} fusion(bf16[1024,1536]{1,0:T(8,128)(2,1)} %get-tuple-element.46, bf16[1024,768]{1,0:T(8,128)(2,1)S(1)} %copy-done.15), kind=kOutput, calls=%fused_computation.3 | convolution fusion | flops 2417098752 | bytes 7077888 | tf_op jit(solution)/shard_map/ti,td->id/dot_general | solution.py:434
  160.9 0.2 reduce-scatter.3.cloned.1.call-start
  161.1 77.9 %layer_backward.1 = (bf16[1024,768]{1,0:T(8,128)(2,1)}, bf16[1024,3328]{1,0:T(8,128)(2,1)}, bf16[1024,128]{1,0:T(8,128)(2,1)}, f32[1,768]{1,0:T(1,128)}, f32[4,1...) custom-call(bf16[1024,768]{1,0:T(8,128)(2,1)} %u_ref.3, ...), custom_call_target="tpu_custom_call" | custom-call | flops 23064477696 | bytes 40000000 | tf_op jit(solution)/shard_map/layer_backward/pallas_call | solution.py:361
  239.1 1.3 convolution_convert_fusion.2
  240.4 0.2 copy.65
  240.6 8.7 %convolution_convert_fusion = bf16[768,3328]{1,0:T(8,128)(2,1)S(1)} fusion(bf16[1024,768]{1,0:T(8,128)(2,1)S(1)} %copy-done, bf16[1024,3328]{1,0:T(8,128)(2,1)} %get-tuple-element.44), kind=kOutput, calls=%fused_computation | convolution fusion | flops 5237047296 | bytes 13500416 | tf_op jit(solution)/shard_map/td,tp->dp/dot_general | solution.py:438
  249.3 2.7 pad_maximum_fusion
  252.1 66.4 %reduce-scatter.3.cloned.1.call-done = bf16[384,3352]{1,0:T(8,128)(2,1)} async-done(((bf16[768,3352]{1,0:T(8,128)(2,1)}), bf16[384,3352]{1,0:T(8,128)(2,1)}) %reduce-scatter.3.cloned.1.call-update) | async-done | bytes 2574352 | tf_op jit(solution)/shard_map/reduce_scatter | solution.py:443
  318.7 0.1 reduce_sum.9
  318.9 0.8 slice_bitcast_fusion
  319.7 0.1 concatenate.22
  319.8 40.7 %psum.21 = f32[11336]{0:T(1024)S(1)} all-reduce(f32[11336]{0:T(1024)S(1)} %concatenate.22), channel_id=1, replica_groups=mesh['shard'=2,'rep'=16] {'shard','rep'}, use_global_device_ids=true, to_apply=%region_1.2 | all-reduce | flops 11336 | bytes 90688 | tf_op jit(solution)/shard_map/psum | solution.py:444
  360.5 0.1 slice.118
  360.6 0.1 fusion.16
  360.6 0.6 dynamic_slice.24
  361.2 0.6 dynamic_slice.25
  361.8 0.6 dynamic_slice.26
  362.4 0.7 dynamic_slice.23
  363.0 0.7 dynamic_slice.27
  363.7 0.6 dynamic_slice.21
  364.4 0.6 constant_dynamic-slice_fusion
  365.0 66.8 %all-reduce.13.cloned.1.call-done = (bf16[384,3352]{1,0:T(8,128)(2,1)}, bf16[768,768]{1,0:T(8,128)(2,1)}) async-done(((bf16[384,3352]{1,0:T(8,128)(2,1)}, bf16[768,768]{1,0:T(8,128)(2,1)}), (bf16[384,3352]{1,0:T(8,128)(2,1)}, bf16[768,768]{1,0:T(8,128)(2,1)})) %all-reduce.13.cloned.1.call-update) | async-done | bytes 3754000 | tf_op jit(solution)/shard_map/psum | solution.py:443
  431.7 4.4 convert_multiply_fusion
  436.1 6.1 %copy.66 = f32[384,3352]{0,1:T(8,128)} copy(f32[384,3352]{1,0:T(8,128)} %convert_multiply_fusion) | data formatting | bytes 10297344
  442.2 1.6 convert_multiply_fusion.1
  (66 shorter events, 0.7 us)
Async XLA Ops:
  7.2 76.7 %all-gather.4.cloned.1.call-start = ((), (), s32[]{:S(2)}) async-start(), calls=%async_computation.2 | async-start | bytes 7962624 | tf_op jit(solution)/shard_map/all_gather | solution.py:416
  11.6 0.9 copy-start.2
  11.6 1.3 copy-start.4
  11.6 1.3 copy-start.16
  11.6 2.6 copy-start.9
  11.6 2.6 copy-start.10
  11.7 2.6 copy-start.11
  11.7 2.6 copy-start.12
  11.7 2.6 copy-start.13
  11.7 2.6 copy-start.14
  11.7 109.8 %all-gather.6.cloned.1.call-start = ((), (), s32[]{:S(2)}) async-start(), calls=%async_computation.3 | async-start | bytes 3538944 | tf_op jit(solution)/shard_map/all_gather | solution.py:417
  12.5 239.6 %reduce-scatter.5.cloned.1.call-start = ((), (), s32[]{:S(2)}) async-start(), calls=%async_computation.5 | async-start | bytes 3538944 | tf_op jit(solution)/shard_map/reduce_scatter | solution.py:435
  121.6 33.3 %copy-start.15 = (bf16[1024,768]{1,0:T(8,128)(2,1)S(1)}, bf16[1024,768]{1,0:T(8,128)(2,1)}, u32[]{:S(2)}) copy-start(bf16[1024,768]{1,0:T(8,128)(2,1)} %g_ref.1) | copy-start | bytes 4718596
  160.9 157.6 %reduce-scatter.3.cloned.1.call-start = ((), (), s32[]{:S(2)}) async-start(), calls=%async_computation.4 | async-start | bytes 7962624 | tf_op jit(solution)/shard_map/reduce_scatter | solution.py:443
  161.1 77.9 %copy-start = (bf16[1024,768]{1,0:T(8,128)(2,1)S(1)}, bf16[1024,768]{1,0:T(8,128)(2,1)}, u32[]{:S(2)}) copy-start(bf16[1024,768]{1,0:T(8,128)(2,1)} %get-tuple-element.43) | copy-start | bytes 4718596
  252.0 66.6 %copy-start.3 = (f32[4,1792]{1,0:T(4,128)S(1)}, f32[4,1792]{1,0:T(4,128)}, u32[]{:S(2)}) copy-start(f32[4,1792]{1,0:T(4,128)} %get-tuple-element.38) | copy-start | bytes 86020
  252.0 66.6 %copy-start.7 = (f32[1,1536]{1,0:T(1,128)S(1)}, f32[1,1536]{1,0:T(1,128)}, u32[]{:S(2)}) copy-start(f32[1,1536]{1,0:T(1,128)} %get-tuple-element.41) | copy-start | bytes 18436
  252.0 66.8 %copy-start.5 = (f32[1,1792]{1,0:T(1,128)S(1)}, f32[1,1792]{1,0:T(1,128)}, u32[]{:S(2)}) copy-start(f32[1,1792]{1,0:T(1,128)} %get-tuple-element.39) | copy-start | bytes 21508
  252.0 66.8 %copy-start.6 = (f32[1,1536]{1,0:T(1,128)S(1)}, f32[1,1536]{1,0:T(1,128)}, u32[]{:S(2)}) copy-start(f32[1,1536]{1,0:T(1,128)} %get-tuple-element.42) | copy-start | bytes 18436
  252.0 66.9 %copy-start.8 = (f32[1,768]{1,0:T(1,128)S(1)}, f32[1,768]{1,0:T(1,128)}, u32[]{:S(2)}) copy-start(f32[1,768]{1,0:T(1,128)} %get-tuple-element.37) | copy-start | bytes 9220
  252.0 179.7 %all-reduce.13.cloned.1.call-start = ((), (), s32[]{:S(2)}) async-start(), calls=%async_computation.6 | async-start | bytes 7667712 | tf_op jit(solution)/shard_map/psum | solution.py:443
  436.1 6.1 %copy-start.1 = (bf16[768,768]{1,0:T(8,128)(2,1)S(1)}, bf16[768,768]{1,0:T(8,128)(2,1)}, u32[]{:S(2)}) copy-start(bf16[768,768]{1,0:T(8,128)(2,1)} %get-tuple-element.92) | copy-start | bytes 3538948
Sparse Core Ops, SparseCore 0:
  11.8 72.0 all-gather.3
  85.5 36.0 all-gather.5
  161.0 34.7 reduce-scatter.4
  252.1 66.3 reduce-scatter.2
  322.6 109.1 all-reduce.12

commit v2 on v1

--- a/solution.py
+++ b/solution.py
@@ -400,10 +400,124 @@
     return layer_out, input_grad, normed, mixed, zx_grad, raw_grad, small
 
 
-def own(full, axis):
-    count = lax.axis_size("shard")
-    size = full.shape[axis] // count
-    return lax.dynamic_slice_in_dim(full, lax.axis_index("shard") * size, size, axis)
+PARTS = 3
+
+
+def gather_kernel(
+    w_in_ref, w_out_ref, vec_ref, w_in_full, w_out_full, vec_full, local_sem, send_sem, recv_sem
+):
+    s, r = lax.axis_index("shard"), lax.axis_index("rep")
+    other = 1 - s
+    core = r % 2
+    side = (r // 2) % 2
+    sibling = r + 1 - 2 * core
+    beside = r + 2 - 4 * side
+    barrier = pltpu.get_barrier_semaphore()
+    for target in ((other, r), (s, beside), (s, sibling)):
+        pl.semaphore_signal(
+            barrier, inc=1, device_id=target, device_id_type=pl.DeviceIdType.MESH
+        )
+    pl.semaphore_wait(barrier, 3)
+
+    def remote(src, dst, index, target):
+        return pltpu.make_async_remote_copy(
+            src_ref=src, dst_ref=dst, send_sem=send_sem.at[index], recv_sem=recv_sem.at[index],
+            device_id=target, device_id_type=pl.DeviceIdType.MESH,
+        )
+
+    vec_rows = vec_ref.shape[0]
+    chunks = []
+    for part in range(PARTS):
+        for src, dst in ((w_in_ref, w_in_full), (w_out_ref, w_out_full)):
+            chunks.append((src, dst, src.shape[0] // 4, src.shape[0] // 4 // PARTS, part))
+    chunks.sort(key=lambda item: item[0] is w_out_ref)
+
+    def place(chunk, shard, quarter):
+        src, _, size, step, part = chunk
+        start = shard * src.shape[0] + quarter * size + part * step
+        return pl.ds(pl.multiple_of(start, 16), step)
+
+    quarter = r % 4
+    beside_quarter = 2 * (1 - side) + core
+    first = []
+    vec_copy = remote(
+        vec_ref, vec_full.at[pl.ds(pl.multiple_of(s * vec_rows, 16), vec_rows), :], 0, (other, r)
+    )
+    vec_copy.start()
+    for n, chunk in enumerate(chunks):
+        copy = remote(
+            chunk[0].at[place(chunk, 0, quarter), :], chunk[1].at[place(chunk, s, quarter), :],
+            1 + 4 * n, (other, r),
+        )
+        copy.start()
+        first.append(copy)
+    local = []
+    for n, (src, dst) in enumerate(
+        ((w_in_ref, w_in_full), (w_out_ref, w_out_full), (vec_ref, vec_full))
+    ):
+        rows = src.shape[0]
+        copy = pltpu.make_async_copy(
+            src, dst.at[pl.ds(pl.multiple_of(s * rows, 16), rows), :], local_sem.at[n]
+        )
+        copy.start()
+        local.append(copy)
+    second, third = [], []
+
+    def pass_on(n):
+        chunk = chunks[n]
+        second[n][0].wait_recv()
+        where = chunk[1].at[place(chunk, other, beside_quarter), :]
+        copy = remote(where, where, 4 + 4 * n, (s, sibling))
+        copy.start()
+        third.append(copy)
+
+    for n, chunk in enumerate(chunks):
+        first[n].wait_recv()
+        where = chunk[1].at[place(chunk, other, quarter), :]
+        sideways = remote(where, where, 2 + 4 * n, (s, beside))
+        sideways.start()
+        across = remote(where, where, 3 + 4 * n, (s, sibling))
+        across.start()
+        second.append((sideways, across))
+        if n > 0:
+            pass_on(n - 1)
+    pass_on(len(chunks) - 1)
+    for n in range(len(chunks)):
+        second[n][1].wait_recv()
+        third[n].wait_recv()
+        first[n].wait_send()
+        second[n][0].wait_send()
+        second[n][1].wait_send()
+        third[n].wait_send()
+    vec_copy.wait()
+    for copy in local:
+        copy.wait()
+
+
+def gather_weights(w_in, w_out, vec):
+    count = 1 + 4 * 2 * PARTS
+    anywhere = pl.BlockSpec(memory_space=pl.ANY)
+    return pl.pallas_call(
+        gather_kernel,
+        in_specs=[anywhere] * 3,
+        out_specs=[anywhere] * 3,
+        out_shape=[
+            jax.ShapeDtypeStruct((2 * a.shape[0], a.shape[1]), a.dtype) for a in (w_in, w_out, vec)
+        ],
+        scratch_shapes=[
+            pltpu.SemaphoreType.DMA((3,)),
+            pltpu.SemaphoreType.DMA((count,)),
+            pltpu.SemaphoreType.DMA((count,)),
+        ],
+        compiler_params=pltpu.CompilerParams(collective_id=0, has_side_effects=True),
+        name="gather_weights",
+    )(w_in, w_out, vec)
+
+
+def by_shard(v):
+    axis = v.ndim - 1
+    cut = v.reshape(v.shape[:axis] + (2, v.shape[axis] // 2))
+    return jnp.moveaxis(cut, axis, 0).reshape(2, -1)
 
 
 def body(
@@ -412,9 +526,10 @@
 ):
     vectors = (norm_gain, conv_weight, conv_bias, dt_bias, a_log, skip_gain, gate_gain)
     packed = jnp.concatenate([v.reshape(-1) for v in vectors])
-    packed = lax.all_gather(packed, "shard", axis=0)
-    w_in = lax.all_gather(in_weight, "shard", axis=0, tiled=True)
-    w_out = lax.all_gather(out_weight, "shard", axis=0, tiled=True)
+    held = packed.size
+    packed = jnp.pad(packed, (0, -held % 2048)).reshape(-1, LANES)
+    w_in, w_out, packed = gather_weights(in_weight, out_weight, packed)
+    packed = packed.reshape(2, -1)
     whole, at = [], 0
     for v in vectors:
         piece = packed[:, at : at + v.size]
@@ -429,27 +544,36 @@
         layer_in, segment_ids.reshape(-1), cotangent, gain, w_in, conv_w, conv_b, step_bias, alog,
         skip, gate_vec, w_out,
     )
-    both = ("shard", "rep")
     factor = 1.0 / (lax.axis_size("shard") * lax.axis_size("rep"))
     out_grad = jnp.einsum("ti,td->id", mixed, cotangent, preferred_element_type=f32).astype(bf16)
     out_sum = lax.psum(lax.psum_scatter(out_grad, "shard", scatter_dimension=0, tiled=True), "rep")
     in_grad = jnp.concatenate(
         [
-            jnp.einsum("td,tp->dp", normed, zx_grad, preferred_element_type=f32),
-            jnp.einsum("td,tp->dp", normed, raw_grad[:, :HEADS], preferred_element_type=f32),
+            jnp.einsum("td,tp->dp", normed, zx_grad, preferred_element_type=f32).astype(bf16),
+            jnp.einsum("td,tp->dp", normed, raw_grad[:, :HEADS], preferred_element_type=f32).astype(
+                bf16
+            ),
         ],
         axis=1,
-    ).astype(bf16)
-    in_sum = lax.psum(lax.psum_scatter(in_grad, "shard", scatter_dimension=0, tiled=True), "rep")
-    flat = lax.psum(jnp.concatenate([v.reshape(-1) for v in small]), both) * factor
+    )
+    rows, proj = in_weight.shape
+    extra = jnp.concatenate([by_shard(v) for v in small], axis=1).astype(bf16)
+    held = extra.shape[1]
+    extra = jnp.pad(extra, ((0, 0), (0, -held % (16 * proj)))).reshape(2, -1, proj)
+    joined = jnp.concatenate([in_grad.reshape(2, rows, proj), extra], axis=1)
+    part = lax.psum_scatter(
+        joined.reshape(-1, proj), "shard", scatter_dimension=0, tiled=True
+    )
+    part, out_sum = lax.optimization_barrier((part, out_sum))
+    in_sum = lax.psum(part, "rep")
+    flat = in_sum[rows:].reshape(-1).astype(f32) * factor
     outs, at = [], 0
-    for v in small:
-        piece = flat[at : at + v.size].reshape(v.shape)
+    for v in vectors:
+        outs.append(flat[at : at + v.size].reshape(v.shape))
         at += v.size
-        outs.append(own(piece, v.ndim - 1))
     return (
-        layer_out, input_grad, outs[0], in_sum.astype(f32) * factor, outs[1], outs[2], outs[3],
-        outs[4], outs[5], outs[6], out_sum.astype(f32) * factor,
+        layer_out, input_grad, outs[0], in_sum[:rows].astype(f32) * factor, outs[1], outs[2],
+        outs[3], outs[4], outs[5], outs[6], out_sum.astype(f32) * factor,
     )
 
 

time: 451 us -> 578 us (1.28)
  Pallas kernels: 111 us -> 232 us
  blocking collectives: 50.5 us -> 0 us
  waiting for transfers between devices: 222 us -> 263 us
  other arithmetic: 12.4 us -> 23.5 us
    psum x1 -> x2, waiting for transfers between devices: 66.8 us -> 192 us  [the longest x1 104 us: body(): in_sum = lax.psum(part, 'rep')]
    pallas_call x0 -> x1, Pallas kernels: none -> 121 us  [gather_weights(): pl.pallas_call(gather_kernel, in_specs=[anywhere] * 3, out_specs=[anywher...]
    all_gather x2 -> x0, waiting for transfers between devices: 87.8 us -> none  [the longest x1 51.8 us: body(): w_in = lax.all_gather(in_weight, 'shard', axis=0, tiled=True)]
    psum x1 -> x0, blocking collectives: 40.7 us -> none  [body(): lax.psum(jnp.concatenate([v.reshape(-1) for v in small]), both) * factor]
    unnamed x1 -> x0, blocking collectives: 9.81 us -> none
    unnamed x45 -> x16, local copies, waits for them, and re-layouts: 14.1 us -> 12.9 us
  transfers between devices with their start and end apart: 5 -> 4, of which waited for: 4 -> 3; matrix products, arithmetic and copies ran while one was open for 6% -> 4% of each run, Pallas kernels for 17% -> 13%
where the time goes in v2:
time: 578 us; the launch traced here: 577 us
  waiting for transfers between devices  263 us (46%)
  Pallas kernels  232 us (40%)
  local copies, waits for them, and re-layouts  28.5 us (5%)
  other arithmetic  23.5 us (4%)
  matrix products  16 us (3%)
  between operations  13.9 us (2%)
    pallas_call x1, Pallas kernels, gather_weights(): pl.pallas_call(gather_kernel, in_specs=[anywhere] * 3, out_specs=[anywher...  121 us
    psum x1, waiting for transfers between devices, body(): in_sum = lax.psum(part, 'rep')  104 us
    psum x1, waiting for transfers between devices, body(): lax.psum(lax.psum_scatter(out_grad, 'shard', scatter_dimension=0, tiled=T...  88.7 us
    pallas_call x1, Pallas kernels, layer(): pl.pallas_call(backward_kernel, grid=(blocks,), in_specs=[rows(width, bwd...  77.9 us
    reduce_scatter x1, waiting for transfers between devices, body(): lax.psum_scatter(joined.reshape(-1, proj), 'shard', scatter_dimension=0,...  70.4 us
    pallas_call x1, Pallas kernels, layer(): pl.pallas_call(forward_kernel, grid=(blocks,), in_specs=[rows(width, fwd)...  33.3 us
    unnamed x16, local copies, waits for them, and re-layouts  12.9 us
  transfers between devices with their start and end apart: 4, of which 3 were waited for; matrix products, arithmetic and copies ran while one was open for 4% of the time, Pallas kernels for 13%

profile of v2, /device:TPU:0, one launch (start us, length us, event | category | flops | bytes accessed | tf_op | source)
XLA Modules:
  0.0 577.5 jit_solution(17427804527590327530)
XLA Ops:
  7.2 1.3 convert_bitcast_fusion.3.seg_ref
  8.5 0.8 slice.89
  9.3 0.8 slice.90
  10.0 0.7 reshape.195
  10.7 4.1 concatenate.22
  14.9 0.6 pad_bitcast_fusion.vec_ref
  15.5 4.4 copy.63.w_in_ref
  19.9 121.1 %gather_weights.1 = (bf16[768,3352]{1,0:T(8,128)(2,1)}, bf16[1536,768]{1,0:T(8,128)(2,1)}, bf16[96,128]{1,0:T(8,128)(2,1)}) custom-call(bf16[384,3352]{1,0:T(8,128)(2,1)} %copy.63.w_in_ref, bf16[768,768]{1,0:T(8,128)(2,1)} %w_out_ref.1, bf16[48,128]{1,0:T(8,128)(2,1)} %pad_bitcast_fusion.vec_ref), custom_call_target="tpu_custom_call" | custom-call | tf_op jit(solution)/shard_map/gather_weights/pallas_call | solution.py:500
  140.9 0.8 reshape.197
  142.0 0.1 pad.64.clone
  142.0 0.1 copy.67
  142.1 0.1 copy.68
  142.3 0.1 iota_compare_fusion
  142.4 0.1 pad_add_fusion
  142.6 0.1 stack.74
  142.8 0.2 copy.62
  143.0 0.8 convert_element_type.136.aux_ref
  143.8 0.9 add_convert_fusion.spread_ref
  144.7 0.1 reshape.217
  144.8 0.1 convert_element_type.148
  144.9 0.1 convert_element_type.147
  145.0 0.6 copy.69
  145.6 0.6 copy.72
  146.2 0.6 copy.71
  146.9 0.7 reshape_reshape.22.skip_ref
  147.5 0.6 copy.70
  148.2 0.9 slice.95
  149.1 0.7 pad.52.step_ref
  149.8 0.7 maximum_maximum_fusion.head_ref
  150.5 33.3 %layer_forward.1 = (bf16[1024,768]{1,0:T(8,128)(2,1)}, f32[1024,1536]{1,0:T(8,128)}, bf16[1024,1792]{1,0:T(8,128)(2,1)}, f32[1024,1792]{1,0:T(8,128)}, f32[1024,...) custom-call(bf16[1024,768]{1,0:T(8,128)(2,1)} %u_ref.3, ...), custom_call_target="tpu_custom_call" | custom-call | flops 15376318464 | bytes 40000000 | tf_op jit(solution)/shard_map/layer_forward/pallas_call | solution.py:328
  183.8 6.0 %convolution_convert_fusion.1 = bf16[1536,768]{1,0:T(8,128)(2,1)} fusion(bf16[1024,1536]{1,0:T(8,128)(2,1)} %get-tuple-element.54, bf16[1024,768]{1,0:T(8,128)(2,1)S(1)} %copy-done.3), kind=kOutput, calls=%fused_computation.4 | convolution fusion | flops 2417098752 | bytes 7077888 | tf_op jit(solution)/shard_map/ti,td->id/dot_general | solution.py:548
  189.8 0.2 all-reduce.14.cloned.1.call-start
  190.1 77.9 %layer_backward.1 = (bf16[1024,768]{1,0:T(8,128)(2,1)}, bf16[1024,3328]{1,0:T(8,128)(2,1)}, bf16[1024,128]{1,0:T(8,128)(2,1)}, f32[1,768]{1,0:T(1,128)}, f32[4,1...) custom-call(bf16[1024,768]{1,0:T(8,128)(2,1)} %u_ref.3, ...), custom_call_target="tpu_custom_call" | custom-call | flops 23064477696 | bytes 40000000 | tf_op jit(solution)/shard_map/layer_backward/pallas_call | solution.py:361
  268.0 0.7 convert_reduce_fusion.2
  268.7 0.7 convert.55
  269.4 0.1 reshape_squeeze.9
  269.5 0.1 reshape_squeeze.8
  269.6 0.7 convert_reduce_fusion
  270.3 0.7 convert_reduce_fusion.1
  271.1 0.7 reduce.4
  271.8 0.1 reduce_sum.9
  272.0 0.1 reshape.202
  272.0 0.8 convert.53
  272.8 1.3 convolution_convert_fusion.2
  274.1 0.2 copy.65
  274.3 0.1 concatenate.26
  274.4 0.1 pad.55
  274.5 0.5 reshape.203
  275.1 8.7 %convolution_convert_fusion = bf16[768,3328]{1,0:T(8,128)(2,1)S(1)} fusion(bf16[1024,768]{1,0:T(8,128)(2,1)S(1)} %copy-done, bf16[1024,3328]{1,0:T(8,128)(2,1)} %get-tuple-element.46), kind=kOutput, calls=%fused_computation | convolution fusion | flops 5237047296 | bytes 13500416 | tf_op jit(solution)/shard_map/td,tp->dp/dot_general | solution.py:552
  283.8 2.8 pad_maximum_fusion.1
  286.6 5.3 pad_maximum_fusion
  292.0 88.7 %all-reduce.14.cloned.1.call-done = bf16[768,768]{1,0:T(8,128)(2,1)} async-done(((bf16[768,768]{1,0:T(8,128)(2,1)}), bf16[768,768]{1,0:T(8,128)(2,1)}) %all-reduce.14.cloned.1.call-update) | async-done | bytes 1179664 | tf_op jit(solution)/shard_map/psum | solution.py:549
  380.7 70.4 %reduce-scatter.3.cloned.1.call-done = bf16[400,3352]{1,0:T(8,128)(2,1)} async-done(((bf16[800,3352]{1,0:T(8,128)(2,1)}), bf16[400,3352]{1,0:T(8,128)(2,1)}) %reduce-scatter.3.cloned.1.call-update) | async-done | bytes 2681616 | tf_op jit(solution)/shard_map/reduce_scatter | solution.py:564
  451.2 1.6 convert_multiply_fusion.1
  452.7 103.7 %all-reduce.16.cloned.1.call-done = bf16[400,3352]{1,0:T(8,128)(2,1)} async-done(((bf16[400,3352]{1,0:T(8,128)(2,1)}), bf16[400,3352]{1,0:T(8,128)(2,1)}) %all-reduce.16.cloned.1.call-update) | async-done | bytes 2681616 | tf_op jit(solution)/shard_map/psum | solution.py:568
  556.4 0.9 convert_multiply_fusion.2
  557.4 0.1 mul.23
  557.5 0.6 fusion.16
  558.1 0.6 slice.122
  558.7 0.7 slice.129
  559.4 0.6 slice.125
  560.0 0.6 reshape.205
  560.6 4.4 convert_multiply_fusion
  565.0 6.0 %copy.66 = f32[384,3352]{0,1:T(8,128)} copy(f32[384,3352]{1,0:T(8,128)} %convert_multiply_fusion) | data formatting | bytes 10297344
  (39 shorter events, 0.9 us)
Async XLA Ops:
  7.2 279.4 %reduce-scatter.5.cloned.1.call-start = ((), (), s32[]{:S(2)}) async-start(), calls=%async_computation.3 | async-start | bytes 3538944 | tf_op jit(solution)/shard_map/reduce_scatter | solution.py:549
  19.9 122.3 %copy-start.2 = (s32[1,1024]{1,0:T(1,128)S(1)}, s32[1,1024]{1,0:T(1,128)}, u32[]{:S(2)}) copy-start(s32[1,1024]{1,0:T(1,128)} %param.13) | copy-start | bytes 12292
  150.5 33.3 %copy-start.3 = (bf16[1024,768]{1,0:T(8,128)(2,1)S(1)}, bf16[1024,768]{1,0:T(8,128)(2,1)}, u32[]{:S(2)}) copy-start(bf16[1024,768]{1,0:T(8,128)(2,1)} %g_ref.1) | copy-start | bytes 4718596
  189.8 190.9 %all-reduce.14.cloned.1.call-start = ((), (), s32[]{:S(2)}) async-start(), calls=%async_computation.4 | async-start | bytes 2359296 | tf_op jit(solution)/shard_map/psum | solution.py:549
  190.1 82.8 %copy-start = (bf16[1024,768]{1,0:T(8,128)(2,1)S(1)}, bf16[1024,768]{1,0:T(8,128)(2,1)}, u32[]{:S(2)}) copy-start(bf16[1024,768]{1,0:T(8,128)(2,1)} %get-tuple-element.45) | copy-start | bytes 4718596
  286.6 164.6 %reduce-scatter.3.cloned.1.call-start = ((), (), s32[]{:S(2)}) async-start(), calls=%async_computation.2 | async-start | bytes 8294400 | tf_op jit(solution)/shard_map/reduce_scatter | solution.py:564
  291.9 264.5 %all-reduce.16.cloned.1.call-start = ((), (), s32[]{:S(2)}) async-start(), calls=%async_computation.5 | async-start | bytes 5529600 | tf_op jit(solution)/shard_map/psum | solution.py:568
  380.7 70.4 %copy-start.1 = (bf16[768,768]{1,0:T(8,128)(2,1)S(1)}, bf16[768,768]{1,0:T(8,128)(2,1)}, u32[]{:S(2)}) copy-start(bf16[768,768]{1,0:T(8,128)(2,1)} %all-reduce.14.cloned.1.call-done) | copy-start | bytes 3538948
Sparse Core Ops, SparseCore 0:
  189.9 35.0 reduce-scatter.4
  286.7 93.9 all-reduce.13
  383.1 67.9 reduce-scatter.2
  455.1 101.3 all-reduce.15

commit v3 on v1

--- a/solution.py
+++ b/solution.py
@@ -82,22 +82,23 @@
 
 
 def forward_kernel(
-    u_ref, aux_ref, seg_ref, gain_ref, in_ref, step_ref, conv_w_ref, conv_b_ref, head_ref, skip_ref,
-    gate_gain_ref, out_w_ref, spread_ref,
+    u_ref, g_ref, aux_ref, seg_ref, gain_ref, in_ref, step_ref, conv_w_ref, conv_b_ref, head_ref,
+    skip_ref, gate_gain_ref, out_w_ref, spread_ref,
     normed_ref, gate_ref, ci_ref, conv_ref, raw_ref, y_ref, state_ref, mixed_ref, out_ref,
+    dgate_gain_ref,
     buf, hidden, y_buf,
 ):
     @pl.when(pl.program_id(0) == 0)
     def _():
         buf[0:8, :] = jnp.zeros((8, XBC), f32)
         hidden[...] = jnp.zeros_like(hidden)
+        dgate_gain_ref[...] = jnp.zeros_like(dgate_gain_ref)
 
     u = u_ref[...].astype(f32)
     inv = lax.rsqrt(jnp.mean(u * u, axis=-1, keepdims=True) + eps)
     normed = (u * inv * gain_ref[...]).astype(bf16)
     normed_ref[...] = normed
     gate = mm(normed, in_ref[:, :INNER])
-    gate_ref[...] = gate
     conv_in = mm(normed, in_ref[:, INNER:WIDE])
     raw = mm(normed, step_ref[...])
     raw_ref[...] = raw
@@ -137,26 +138,33 @@
     hidden[...] = state * enter_wide[BLOCK - 1 :, :] + mm(
         b_low, (weighted * leave_wide).astype(bf16), ((0,), (0,))
     )
-    y_ref[...] = y
-    gated = y * (gate * sigmoid(gate))
+    gate_sig = sigmoid(gate)
+    gate_act = gate * gate_sig
+    gated = y * gate_act
     inv_g = lax.rsqrt(jnp.mean(gated * gated, axis=-1, keepdims=True) + eps)
     mixed = (gated * inv_g * gate_gain_ref[...]).astype(bf16)
     mixed_ref[...] = mixed
     out_ref[...] = (u + mm(mixed, out_w_ref[...])).astype(bf16)
+    mixed_grad = mm(g_ref[...], out_w_ref[...], ((1,), (1,)))
+    dgate_gain_ref[...] += jnp.sum(mixed_grad * gated * inv_g, axis=0, keepdims=True)
+    scaled = mixed_grad * gate_gain_ref[...]
+    mean_term = jnp.mean(scaled * gated, axis=-1, keepdims=True)
+    d_gated = inv_g * scaled - gated * (inv_g * inv_g * inv_g * mean_term)
+    y_ref[...] = d_gated * gate_act
+    gate_ref[...] = (d_gated * y * (gate_sig * (1.0 + gate * (1.0 - gate_sig)))).astype(bf16)
 
 
 def backward_kernel(
     u_ref, g_ref, aux_ref, seg_ref, gain_ref, in_ref, step_ref, conv_w_ref, head_ref, skip_ref,
-    gate_gain_ref, out_w_ref, spread_ref, gate_ref, ci_ref, conv_ref, raw_ref, y_ref, state_ref,
+    spread_ref, gate_ref, ci_ref, conv_ref, raw_ref, y_ref, state_ref,
     ingrad_ref, zx_ref, rawg_ref, dgain_ref, dconv_w_ref, dconv_b_ref, dhead_ref, dskip_ref,
-    dgate_gain_ref,
     buf, d_hidden, dw_buf,
 ):
     @pl.when(pl.program_id(0) == 0)
     def _():
         buf[BLOCK:, :] = jnp.zeros((8, XBC), f32)
         d_hidden[...] = jnp.zeros_like(d_hidden)
-        for ref in (dgain_ref, dconv_w_ref, dconv_b_ref, dhead_ref, dskip_ref, dgate_gain_ref):
+        for ref in (dgain_ref, dconv_w_ref, dconv_b_ref, dhead_ref, dskip_ref):
             ref[...] = jnp.zeros_like(ref)
 
     def total(v):
@@ -165,20 +173,7 @@
     g = g_ref[...]
     aux = aux_ref[...]
     spread_mat = spread_ref[...]
-    mixed_grad = mm(g, out_w_ref[...], ((1,), (1,)))
-    gate = gate_ref[...]
-    y = y_ref[...]
-    gate_sig = sigmoid(gate)
-    gate_act = gate * gate_sig
-    gated = y * gate_act
-    inv_g = lax.rsqrt(jnp.mean(gated * gated, axis=-1, keepdims=True) + eps)
-    dgate_gain_ref[...] += total(mixed_grad * gated * inv_g)
-    scaled = mixed_grad * gate_gain_ref[...]
-    mean_term = jnp.mean(scaled * gated, axis=-1, keepdims=True)
-    d_gated = inv_g * scaled - gated * (inv_g * inv_g * inv_g * mean_term)
-    dy = d_gated * gate_act
-    zx_ref[:, :INNER] = (d_gated * y * (gate_sig * (1.0 + gate * (1.0 - gate_sig)))).astype(bf16)
-
+    dy = y_ref[...]
     conv = conv_ref[...]
     conv_sig = sigmoid(conv)
     active = conv * conv_sig
@@ -267,9 +262,12 @@
         d_in = d_in + conv_w_ref[3 - k : 4 - k, :] * later
         dconv_w_ref[3 - k : 4 - k, :] += total(conv_in * later)
     buf[BLOCK:, :] = d_conv[:8, :]
-    zx_ref[:, INNER:] = d_in.astype(bf16)
-    normed_grad = mm(zx_ref[...], in_ref[:, :WIDE], ((1,), (1,))) + mm(
-        raw_low, step_ref[...], ((1,), (1,))
+    d_in_low = d_in.astype(bf16)
+    zx_ref[...] = d_in_low
+    normed_grad = (
+        mm(gate_ref[...], in_ref[:, :INNER], ((1,), (1,)))
+        + mm(d_in_low, in_ref[:, INNER:WIDE], ((1,), (1,)))
+        + mm(raw_low, step_ref[...], ((1,), (1,)))
     )
     u = u_ref[...].astype(f32)
     inv = lax.rsqrt(jnp.mean(u * u, axis=-1, keepdims=True) + eps)
@@ -325,24 +323,24 @@
     params = pltpu.CompilerParams(
         dimension_semantics=("arbitrary",), vmem_limit_bytes=60 * 1024 * 1024
     )
-    normed, gate, conv_in, conv, raw, y, states, mixed, layer_out = pl.pallas_call(
+    normed, gate, conv_in, conv, raw, y, states, mixed, layer_out, d_gate_gain = pl.pallas_call(
         forward_kernel,
         grid=(blocks,),
         in_specs=[
-            rows(width, fwd), rows(16, fwd), pl.BlockSpec((1, 1, BLOCK), lambda i: (i, 0, 0)),
+            rows(width, fwd), rows(width, fwd), rows(16, fwd), pl.BlockSpec((1, 1, BLOCK), lambda i: (i, 0, 0)),
             full(gain_row), full(w_in), full(w_step), full(conv_w), full(conv_b), full(heads),
             full(skip_wide), full(gate_row), full(w_out), full(spread_mat),
         ],
         out_specs=[
             rows(width, fwd), rows(INNER, fwd), rows(XBC, fwd), rows(XBC, fwd), rows(LANES, fwd),
             rows(INNER, fwd), pl.BlockSpec((1, STATE, INNER), lambda i: (i, 0, 0)),
-            rows(INNER, fwd), rows(width, fwd),
+            rows(INNER, fwd), rows(width, fwd), pl.BlockSpec((1, INNER), lambda i: (0, 0)),
         ],
         out_shape=[
-            shape((tokens, width), bf16), shape((tokens, INNER), f32), shape((tokens, XBC), bf16),
+            shape((tokens, width), bf16), shape((tokens, INNER), bf16), shape((tokens, XBC), bf16),
             shape((tokens, XBC), f32), shape((tokens, LANES), f32), shape((tokens, INNER), f32),
             shape((blocks, STATE, INNER), bf16), shape((tokens, INNER), bf16),
-            shape((tokens, width), bf16),
+            shape((tokens, width), bf16), shape((1, INNER), f32),
         ],
         scratch_shapes=[
             pltpu.VMEM((BLOCK + 8, XBC), f32), pltpu.VMEM((STATE, INNER), f32),
@@ -354,10 +352,10 @@
             transcendentals=tokens * 8000,
         ),
         name="layer_forward",
-    )(layer_in, aux, seg_rows, gain_row, w_in, w_step, conv_w, conv_b, heads, skip_wide, gate_row,
+    )(layer_in, cotangent, aux, seg_rows, gain_row, w_in, w_step, conv_w, conv_b, heads, skip_wide, gate_row,
       w_out, spread_mat)
     acc = lambda r, c: pl.BlockSpec((r, c), lambda i: (0, 0))
-    input_grad, zx_grad, raw_grad, d_gain, d_conv_w, d_conv_b, d_heads, d_skip, d_gate_gain = (
+    input_grad, zx_grad, raw_grad, d_gain, d_conv_w, d_conv_b, d_heads, d_skip = (
         pl.pallas_call(
             backward_kernel,
             grid=(blocks,),
@@ -365,20 +363,19 @@
                 rows(width, bwd), rows(width, bwd), rows(16, bwd),
                 pl.BlockSpec((1, 1, BLOCK), lambda i: (blocks - 1 - i, 0, 0)),
                 full(gain_row), full(w_in), full(w_step), full(conv_w), full(heads),
-                full(skip_wide), full(gate_row), full(w_out), full(spread_mat),
+                full(skip_wide), full(spread_mat),
                 rows(INNER, bwd), rows(XBC, bwd), rows(XBC, bwd), rows(LANES, bwd),
                 rows(INNER, bwd),
                 pl.BlockSpec((1, STATE, INNER), lambda i: (blocks - 1 - i, 0, 0)),
             ],
             out_specs=[
-                rows(width, bwd), rows(WIDE, bwd), rows(LANES, bwd), acc(1, width), acc(CONV, XBC),
-                acc(1, XBC), acc(8, LANES), acc(1, INNER), acc(1, INNER),
+                rows(width, bwd), rows(XBC, bwd), rows(LANES, bwd), acc(1, width), acc(CONV, XBC),
+                acc(1, XBC), acc(8, LANES), acc(1, INNER),
             ],
             out_shape=[
-                shape((tokens, width), bf16), shape((tokens, WIDE), bf16),
+                shape((tokens, width), bf16), shape((tokens, XBC), bf16),
                 shape((tokens, LANES), bf16), shape((1, width), f32), shape((CONV, XBC), f32),
                 shape((1, XBC), f32), shape((8, LANES), f32), shape((1, INNER), f32),
-                shape((1, INNER), f32),
             ],
             scratch_shapes=[
                 pltpu.VMEM((BLOCK + 8, XBC), f32), pltpu.VMEM((STATE, INNER), f32),
@@ -391,13 +388,13 @@
             ),
             name="layer_backward",
         )(layer_in, cotangent, aux, seg_rows, gain_row, w_in, w_step, conv_w, heads, skip_wide,
-          gate_row, w_out, spread_mat, gate, conv_in, conv, raw, y, states)
+          spread_mat, gate, conv_in, conv, raw, y, states)
     )
     small = (
         d_gain.reshape(width), d_conv_w, d_conv_b.reshape(XBC), d_heads[0, :HEADS],
         d_heads[1, :HEADS], d_skip.reshape(HEADS, HEADDIM).sum(axis=1), d_gate_gain.reshape(INNER),
     )
-    return layer_out, input_grad, normed, mixed, zx_grad, raw_grad, small
+    return layer_out, input_grad, normed, mixed, gate, zx_grad, raw_grad, small
 
 
 def own(full, axis):
@@ -425,22 +422,26 @@
             piece = piece.reshape(-1)
         whole.append(piece)
     gain, conv_w, conv_b, step_bias, alog, skip, gate_vec = whole
-    layer_out, input_grad, normed, mixed, zx_grad, raw_grad, small = layer(
+    layer_out, input_grad, normed, mixed, gate_grad, zx_grad, raw_grad, small = layer(
         layer_in, segment_ids.reshape(-1), cotangent, gain, w_in, conv_w, conv_b, step_bias, alog,
         skip, gate_vec, w_out,
     )
     both = ("shard", "rep")
     factor = 1.0 / (lax.axis_size("shard") * lax.axis_size("rep"))
     out_grad = jnp.einsum("ti,td->id", mixed, cotangent, preferred_element_type=f32).astype(bf16)
-    out_sum = lax.psum(lax.psum_scatter(out_grad, "shard", scatter_dimension=0, tiled=True), "rep")
-    in_grad = jnp.concatenate(
+    early = jnp.einsum("td,tp->dp", normed, gate_grad, preferred_element_type=f32).astype(bf16)
+    early, out_sum = lax.psum((early, out_grad), both)
+    late = jnp.concatenate(
         [
             jnp.einsum("td,tp->dp", normed, zx_grad, preferred_element_type=f32),
             jnp.einsum("td,tp->dp", normed, raw_grad[:, :HEADS], preferred_element_type=f32),
         ],
         axis=1,
     ).astype(bf16)
-    in_sum = lax.psum(lax.psum_scatter(in_grad, "shard", scatter_dimension=0, tiled=True), "rep")
+    late, early, out_sum = lax.optimization_barrier((late, early, out_sum))
+    late = lax.psum(late, both)
+    in_sum = jnp.concatenate([own(early, 0), own(late, 0)], axis=1)
+    out_sum = own(out_sum, 0)
     flat = lax.psum(jnp.concatenate([v.reshape(-1) for v in small]), both) * factor
     outs, at = [], 0
     for v in small:

time: 451 us -> 479 us (1.062)
  waiting for transfers between devices: 222 us -> 255 us
  Pallas kernels: 111 us -> 103 us
    psum x1 -> x2, waiting for transfers between devices: 66.8 us -> 166 us  [the longest x1 94.5 us: body(): late = lax.psum(late, both)]
    reduce_scatter x2 -> x0, waiting for transfers between devices: 66.4 us -> none  [the longest x1 66.4 us: body(): lax.psum_scatter(in_grad, 'shard', scatter_dimension=0, tiled=True)]
    pallas_call x1, Pallas kernels: 77.9 us -> 61.3 us  [layer(): pl.pallas_call(backward_kernel, grid=(blocks,), in_specs=[rows(width, bwd...]
    pallas_call x1, Pallas kernels: 33.3 us -> 42 us  [layer(): pl.pallas_call(forward_kernel, grid=(blocks,), in_specs=[rows(width, fwd)...]
    unnamed x45 -> x39, local copies, waits for them, and re-layouts: 14.1 us -> 14 us
  transfers between devices with their start and end apart: 5 -> 4, of which waited for: 4 -> 4; matrix products, arithmetic and copies ran while one was open for 6% -> 6% of each run, Pallas kernels for 17% -> 13%
where the time goes in v3:
time: 479 us; the launch traced here: 478 us
  waiting for transfers between devices  255 us (53%)
  Pallas kernels  103 us (22%)
  blocking collectives  49.5 us (10%)
  local copies, waits for them, and re-layouts  25.6 us (5%)
  matrix products  16.7 us (3%)
  between operations  14.8 us (3%)
  other arithmetic  13.1 us (3%)
    psum x1, waiting for transfers between devices, body(): late = lax.psum(late, both)  94.5 us
    psum x1, waiting for transfers between devices, body(): early, out_sum = lax.psum((early, out_grad), both)  71.8 us
    pallas_call x1, Pallas kernels, layer(): pl.pallas_call(backward_kernel, grid=(blocks,), in_specs=[rows(width, bwd...  61.3 us
    all_gather x1, waiting for transfers between devices, body(): w_in = lax.all_gather(in_weight, 'shard', axis=0, tiled=True)  51.7 us
    pallas_call x1, Pallas kernels, layer(): pl.pallas_call(forward_kernel, grid=(blocks,), in_specs=[rows(width, fwd)...  42 us
    psum x1, blocking collectives, body(): lax.psum(jnp.concatenate([v.reshape(-1) for v in small]), both) * factor  39.7 us
    all_gather x1, waiting for transfers between devices, body(): w_out = lax.all_gather(out_weight, 'shard', axis=0, tiled=True)  36 us
    unnamed x39, local copies, waits for them, and re-layouts  14 us
  transfers between devices with their start and end apart: 4, of which 4 were waited for; matrix products, arithmetic and copies ran while one was open for 6% of the time, Pallas kernels for 13%

profile of v3, /device:TPU:0, one launch (start us, length us, event | category | flops | bytes accessed | tf_op | source)
XLA Modules:
  0.0 478.0 jit_solution(15606020899437812274)
XLA Ops:
  7.2 4.4 copy.63
  11.8 0.7 all-gather.6.cloned.1.call-update
  12.7 0.1 fusion.10
  12.8 0.1 copy.68
  12.8 0.1 copy.67
  13.0 0.6 dynamic-slice
  14.3 0.1 concatenate.22
  14.4 0.4 dynamic-update-slice
  14.7 9.8 %all-reduce.9 = bf16[11336]{0:T(1024)(128)(2,1)S(1)} all-reduce(bf16[11336]{0:T(1024)(128)(2,1)S(1)} %dynamic-update-slice), channel_id=2, replica_groups=mesh['shard'=2,'rep'=16] {'shard'}, use_global_device_ids=true, to_apply=%add.9 | all-reduce | flops 11336 | bytes 45344
  24.5 0.1 reshape.197
  24.7 0.1 pad_add_fusion
  24.9 0.1 stack.74
  25.0 0.2 copy.62
  25.2 0.9 convert_element_type.125.aux_ref
  26.1 0.6 copy.69
  26.7 0.6 copy.70
  27.3 0.6 copy.71
  28.0 0.1 convert_element_type.137
  28.1 0.1 convert_element_type.136
  28.2 0.1 pad.55.clone
  28.3 0.1 pad.54.clone
  28.3 0.1 reshape.194
  28.5 0.7 reshape_reshape.10.skip_ref
  29.2 0.1 convert_bitcast_fusion.2
  29.3 0.6 copy.72
  29.9 0.7 maximum_maximum_fusion.head_ref
  30.5 0.6 convert_bitcast_fusion.3.seg_ref
  31.1 0.1 iota_compare_fusion
  31.2 0.9 add_convert_fusion.spread_ref
  32.2 51.7 %all-gather.4.cloned.1.call-done.in_ref = bf16[768,3352]{1,0:T(8,128)(2,1)} async-done(((bf16[384,3352]{1,0:T(8,128)(2,1)}), bf16[768,3352]{1,0:T(8,128)(2,1)}) %all-gather.4.cloned.1.call-update) | async-done | bytes 5148688 | tf_op jit(solution)/shard_map/all_gather | solution.py:413
  83.9 0.9 slice.105
  84.9 0.7 pad.43.step_ref
  85.6 36.0 %all-gather.6.cloned.1.call-done.out_w_ref = bf16[1536,768]{1,0:T(8,128)(2,1)} async-done(((bf16[768,768]{1,0:T(8,128)(2,1)}), bf16[1536,768]{1,0:T(8,128)(2,1)}) %all-gather.6.cloned.1.call-update) | async-done | bytes 2359312 | tf_op jit(solution)/shard_map/all_gather | solution.py:414
  121.6 42.0 %layer_forward.1 = (bf16[1024,768]{1,0:T(8,128)(2,1)}, bf16[1024,1536]{1,0:T(8,128)(2,1)}, bf16[1024,1792]{1,0:T(8,128)(2,1)}, f32[1024,1792]{1,0:T(8,128)}, f32...) custom-call(bf16[1024,768]{1,0:T(8,128)(2,1)} %u_ref.3, ...), custom_call_target="tpu_custom_call" | custom-call | flops 15376318464 | bytes 40000000 | tf_op jit(solution)/shard_map/layer_forward/pallas_call | solution.py:326
  163.7 6.1 %convolution_convert_fusion = bf16[1536,768]{1,0:T(8,128)(2,1)} fusion(bf16[1024,1536]{1,0:T(8,128)(2,1)} %get-tuple-element.49, bf16[1024,768]{1,0:T(8,128)(2,1)S(1)} %copy-done.11), kind=kOutput, calls=%fused_computation.1 | convolution fusion | flops 2417098752 | bytes 7077888 | tf_op jit(solution)/shard_map/ti,td->id/dot_general | solution.py:431
  169.8 3.9 convolution_convert_fusion.1
  173.7 0.2 all-reduce.14.cloned.1.call-start
  173.9 61.3 %layer_backward.1 = (bf16[1024,768]{1,0:T(8,128)(2,1)}, bf16[1024,1792]{1,0:T(8,128)(2,1)}, bf16[1024,128]{1,0:T(8,128)(2,1)}, f32[1,768]{1,0:T(1,128)}, f32[4,1...) custom-call(bf16[1024,768]{1,0:T(8,128)(2,1)} %u_ref.3, bf16[1024,768]{1,0:T(8,128)(2,1)} %g_ref.3, ...), custom_call_target="tpu_custom_call" | custom-call | flops 23064477696 | bytes 40000000 | tf_op jit(solution)/shard_map/layer_backward/pallas_call | solution.py:359
  235.2 0.8 reshape.178
  236.0 0.7 reduce
  236.7 0.7 reduce.1
  237.4 0.7 reduce.2
  238.2 0.1 reduce_sum.9
  238.3 1.3 convolution_convert_fusion.3
  239.6 0.2 copy.65
  239.8 5.4 %convolution_convert_fusion.2 = bf16[768,1792]{1,0:T(8,128)(2,1)S(1)} fusion(bf16[1024,768]{1,0:T(8,128)(2,1)S(1)} %copy-done, bf16[1024,1792]{1,0:T(8,128)(2,1)} %get-tuple-element.47), kind=kOutput, calls=%fused_computation.3 | convolution fusion | flops 2819948544 | bytes 7995392 | tf_op jit(solution)/shard_map/td,tp->dp/dot_general | solution.py:436
  245.2 1.8 pad_maximum_fusion
  247.0 71.8 %all-reduce.16.cloned.1.call-done = (bf16[768,1536]{1,0:T(8,128)(2,1)}, bf16[1536,768]{1,0:T(8,128)(2,1)}) async-done(((bf16[768,1536]{1,0:T(8,128)(2,1)}, bf16[1536,768]{1,0:T(8,128)(2,1)}), (bf16[768,1536]{1,0:T(8,128)(2,1)}, bf16[1536,768]{1,0:T(8,128)(2,1)})) %all-reduce.16.cloned.1.call-update) | async-done | bytes 4718608 | tf_op jit(solution)/shard_map/psum | solution.py:433
  318.8 0.8 slice_bitcast_fusion
  319.6 0.1 concatenate.25
  319.7 39.7 %psum.28 = f32[11336]{0:T(1024)S(1)} all-reduce(f32[11336]{0:T(1024)S(1)} %concatenate.25), channel_id=1, replica_groups=mesh['shard'=2,'rep'=16] {'shard','rep'}, use_global_device_ids=true, to_apply=%region_1.2 | all-reduce | flops 11336 | bytes 90688 | tf_op jit(solution)/shard_map/psum | solution.py:445
  359.6 0.6 dynamic_slice.35
  360.2 0.6 dynamic_slice.36
  360.8 0.6 dynamic_slice.37
  361.3 0.6 dynamic_slice.30
  362.0 0.7 dynamic_slice.34
  362.7 0.7 dynamic_slice.38
  363.3 0.6 constant_dynamic-slice_fusion
  363.9 2.8 convert_multiply_fusion.1
  366.8 0.1 constant_dynamic-slice_fusion.2
  366.8 94.5 %all-reduce.14.cloned.1.call-done = bf16[768,1816]{1,0:T(8,128)(2,1)} async-done(((bf16[768,1816]{1,0:T(8,128)(2,1)}), bf16[768,1816]{1,0:T(8,128)(2,1)}) %all-reduce.14.cloned.1.call-update) | async-done | bytes 2789392 | tf_op jit(solution)/shard_map/psum | solution.py:442
  461.3 1.5 constant_dynamic-slice_fusion.1
  462.8 2.7 convert_multiply_fusion
  465.5 6.0 %copy.66 = f32[384,3352]{0,1:T(8,128)} copy(f32[384,3352]{1,0:T(8,128)} %convert_multiply_fusion) | data formatting | bytes 10297344
  (60 shorter events, 1.0 us)
Async XLA Ops:
  7.2 76.7 %all-gather.4.cloned.1.call-start = ((), (), s32[]{:S(2)}) async-start(), calls=%async_computation | async-start | bytes 7962624 | tf_op jit(solution)/shard_map/all_gather | solution.py:413
  11.6 0.9 copy-start.1
  11.6 1.3 copy-start.3
  11.6 1.3 copy-start.12
  11.6 2.6 copy-start.5
  11.6 2.6 copy-start.6
  11.7 2.6 copy-start.7
  11.7 2.6 copy-start.8
  11.7 2.6 copy-start.9
  11.7 2.6 copy-start.10
  11.7 109.8 %all-gather.6.cloned.1.call-start = ((), (), s32[]{:S(2)}) async-start(), calls=%async_computation.1 | async-start | bytes 3538944 | tf_op jit(solution)/shard_map/all_gather | solution.py:414
  12.5 306.3 %all-reduce.16.cloned.1.call-start = ((), (), s32[]{:S(2)}) async-start(), calls=%async_computation.3 | async-start | bytes 9437184 | tf_op jit(solution)/shard_map/psum | solution.py:433
  121.6 42.1 %copy-start.11 = (bf16[1024,768]{1,0:T(8,128)(2,1)S(1)}, bf16[1024,768]{1,0:T(8,128)(2,1)}, u32[]{:S(2)}) copy-start(bf16[1024,768]{1,0:T(8,128)(2,1)} %g_ref.3) | copy-start | bytes 4718596
  163.6 6.1 %copy-start = (bf16[1024,768]{1,0:T(8,128)(2,1)S(1)}, bf16[1024,768]{1,0:T(8,128)(2,1)}, u32[]{:S(2)}) copy-start(bf16[1024,768]{1,0:T(8,128)(2,1)} %get-tuple-element.46) | copy-start | bytes 4718596
  163.7 6.1 %copy-start.13 = (bf16[1024,1536]{1,0:T(8,128)(2,1)S(1)}, bf16[1024,1536]{1,0:T(8,128)(2,1)}, u32[]{:S(2)}) copy-start(bf16[1024,1536]{1,0:T(8,128)(2,1)} %get-tuple-element.33.gate_ref) | copy-start | bytes 9437188
  173.7 287.6 %all-reduce.14.cloned.1.call-start = ((), (), s32[]{:S(2)}) async-start(), calls=%async_computation.2 | async-start | bytes 5898240 | tf_op jit(solution)/shard_map/psum | solution.py:442
  173.9 64.4 %copy-start.4 = (f32[1,1536]{1,0:T(1,128)S(1)}, f32[1,1536]{1,0:T(1,128)}, u32[]{:S(2)}) copy-start(f32[1,1536]{1,0:T(1,128)} %get-tuple-element.45) | copy-start | bytes 18436
  318.8 48.0 %copy-start.2 = (bf16[768,1536]{1,0:T(8,128)(2,1)S(1)}, bf16[768,1536]{1,0:T(8,128)(2,1)}, u32[]{:S(2)}) copy-start(bf16[768,1536]{1,0:T(8,128)(2,1)} %get-tuple-element.50) | copy-start | bytes 7077892
Sparse Core Ops, SparseCore 0:
  11.8 72.0 all-gather.3
  85.5 36.0 all-gather.5
  173.8 144.8 all-reduce.15
  325.6 135.6 all-reduce.13
